TPU v7x, 1024 devices: a whole 4x8x16 slice. The times are simulated.
1024 devices in a mesh: ctx: 128 (over y, z), head: 8 (over x, core).
Axes of the slice: x: 4, y: 8, z: 16, core: 2. Of those that a mesh axis runs over, the one named last changes fastest.
Arguments:
- seq_inputs: bfloat16 [32768, 5120], P('ctx', 'head'), may hold values from -0.4375 to 0.4375
- state_write: bfloat16 [32768, 128], P('ctx'), may hold values from -2 to 2
- state_read: bfloat16 [32768, 128], P('ctx'), may hold values from -2 to 2
- log_decay: float32 [80, 32768], P('head', 'ctx'), may hold values from -1 to 0
- level_weight: int32 [8, 80, 32768], P(None, 'head', 'ctx'), may hold values from 1 to 16
- grad_out: bfloat16 [32768, 5120], P('ctx', 'head'), may hold values from -0.4375 to 0.4375
Outputs:
- mixer_out: bfloat16 [32768, 5120], P('ctx', 'head')
- grad_inputs: bfloat16 [32768, 5120], P('ctx', 'head')
- grad_write: float32 [32768, 128], P(('ctx', 'head'))
- grad_read: float32 [32768, 128], P(('ctx', 'head'))
All inputs are finite; a program needn't handle non-finite values.
Results may differ from a plain program's by a relative error of at most 0.0064.
Values sent between devices are 32-bit elements; how exact they have to be, the bound alone decides.
No kernel may reach another device: no remote copies, remote signals or barrier semaphores. Data moves between devices by JAX's collectives and lax.ppermute only.
A program may use at most 32 MiB of HBM per device.

v0:
```python
import jax
import jax.numpy as jnp
from jax import lax
from jax.sharding import PartitionSpec as P


def from_partner(value, axis, stride):
    mask = 2**stride
    pairs = [(source, source ^ mask) for source in range(lax.axis_size(axis))]
    return lax.ppermute(value, axis, pairs)


def split_up(value, dim, count):
    shape = value.shape
    pieces = value.reshape(*shape[:dim], count, shape[dim] // count, *shape[dim + 1 :])
    return jnp.moveaxis(pieces, dim, 0)


def sum_at_owner(value, axis, dim):
    pieces = split_up(value, dim, lax.axis_size(axis))
    arrived = lax.all_to_all(pieces, axis, split_axis=0, concat_axis=0, tiled=True)
    return arrived.sum(axis=0)


def side_by_side(arrays, axis, dim, along):
    ends, at = ([], 0)
    for a in arrays[:-1]:
        at += a.shape[along]
        ends.append(at)
    both = jnp.concatenate(arrays, axis=along)
    return tuple(jnp.split(sum_at_owner(both, axis, dim), ends, axis=along))


def climb_levels(state, total, shard_index, level_count):
    block_state = state
    block_span = total
    offset = jnp.zeros_like(total)
    buckets, offsets, own_states, own_spans, peer_spans = ([], [], [], [], [])
    for level_bit in range(level_count):
        peer_state, peer_span = from_partner((block_state, block_span), "ctx", level_bit)
        divisor = 2**level_bit
        is_right = shard_index // divisor % 2 == 1
        buckets.append(peer_state)
        offsets.append(offset)
        own_states.append(block_state)
        own_spans.append(block_span)
        peer_spans.append(peer_span)
        offset = offset + jnp.where(is_right, peer_span, 0.0)
        if level_bit + 1 < level_count:
            block_state = jnp.where(
                is_right,
                jnp.exp(block_span)[:, None, None] * peer_state + block_state,
                jnp.exp(peer_span)[:, None, None] * block_state + peer_state,
            )
        block_span = block_span + peer_span
    return (buckets, offsets, own_states, own_spans, peer_spans)


def descend(make_grad, level_count, own_states, own_spans, peer_spans, shard_index, dread_start):
    carried = None
    dread_far = dread_start
    for level_bit in reversed(range(level_count)):
        level_grad, weighted = make_grad(level_bit)
        if carried is None:
            carried = jnp.zeros_like(level_grad)
        divisor = 2**level_bit
        is_right = shard_index // divisor % 2 == 1
        outgoing = jnp.where(
            is_right, jnp.exp(own_spans[level_bit])[:, None, None] * carried + level_grad, carried
        )
        incoming, peer_block = from_partner((outgoing, own_states[level_bit]), "ctx", level_bit)
        dread_part = jnp.einsum(
            "thp,hpn->tn", weighted.astype(jnp.float32), peer_block, precision=lax.Precision.HIGHEST
        )
        dread_far = dread_far + dread_part
        carried = (
            jnp.where(is_right, carried, jnp.exp(peer_spans[level_bit])[:, None, None] * carried)
            + incoming
        )
    return (carried, dread_far)


def body(seq_inputs, state_write, state_read, log_decay, level_weight, grad_out):
    row_count = seq_inputs.shape[0]
    head_count = log_decay.shape[0]
    head_width = seq_inputs.shape[1] // head_count
    inputs = seq_inputs.reshape(row_count, head_count, head_width)
    cotangent = grad_out.reshape(row_count, head_count, head_width)
    scaled = level_weight.astype(jnp.float32) * 0.125
    running = jnp.cumsum(log_decay, axis=1)
    total = running[:, -1]
    scores = jnp.dot(state_read, state_write.T, preferred_element_type=jnp.float32)
    token_positions = jnp.arange(row_count)
    causal = (token_positions[:, None] >= token_positions[None, :])[None]
    gaps = running[:, :, None] - running[:, None, :]
    local_weight = (
        jnp.where(causal, jnp.exp(jnp.where(causal, gaps, 0.0)), 0.0) * scaled[0][:, :, None]
    )
    mixing = (local_weight * scores[None]).astype(jnp.bfloat16)
    y_local = jnp.einsum("htu,uhp->thp", mixing, inputs, preferred_element_type=jnp.float32)
    to_end = jnp.exp(total[:, None] - running)
    written = (to_end[:, :, None] * state_write.astype(jnp.float32)[None]).astype(jnp.bfloat16)
    state = jnp.einsum("uhp,hun->hpn", inputs, written, preferred_element_type=jnp.float32)
    shard_index = lax.axis_index("ctx")
    level_count = lax.axis_size("ctx").bit_length() - 1
    buckets, offsets, own_states, own_spans, peer_spans = climb_levels(
        state, total, shard_index, level_count
    )
    read_wide = state_read.astype(jnp.float32)
    y_far = jnp.zeros((row_count, head_count, head_width), jnp.float32)
    coefficients = []
    for level_bit in range(level_count):
        divisor = 2**level_bit
        is_right = shard_index // divisor % 2 == 1
        coeff = jnp.where(
            is_right, scaled[level_bit + 1] * jnp.exp(running + offsets[level_bit][:, None]), 0.0
        )
        coeff_rows = coeff.T[:, :, None]
        raw = jnp.einsum(
            "tn,hpn->thp", read_wide, buckets[level_bit], precision=lax.Precision.HIGHEST
        )
        y_far = y_far + raw * coeff_rows
        coefficients.append(coeff_rows)
    mixer_out = (y_local + y_far).astype(jnp.bfloat16).reshape(row_count, head_count * head_width)
    d_mixing = jnp.einsum("thp,uhp->htu", cotangent, inputs, preferred_element_type=jnp.float32)
    d_scores = (d_mixing * local_weight).astype(jnp.bfloat16)
    dread_local = jnp.einsum(
        "htu,un->tn", d_scores, state_write, preferred_element_type=jnp.float32
    )
    dwrite_local = jnp.einsum(
        "htu,tn->un", d_scores, state_read, preferred_element_type=jnp.float32
    )
    dinput_local = jnp.einsum("htu,thp->uhp", mixing, cotangent, preferred_element_type=jnp.float32)

    def level_terms(level_bit):
        weighted = (coefficients[level_bit] * cotangent.astype(jnp.float32)).astype(jnp.bfloat16)
        level_grad = jnp.einsum(
            "thp,tn->hpn", weighted, state_read, preferred_element_type=jnp.float32
        )
        return (level_grad, weighted)

    dread_zero = jnp.zeros((row_count, state_read.shape[1]), jnp.float32)
    prepared = [level_terms(level_bit) for level_bit in range(level_count)]

    def make_grad(level_bit):
        return prepared[level_bit]

    dstate, dread_far = descend(
        make_grad, level_count, own_states, own_spans, peer_spans, shard_index, dread_zero
    )
    dstate_low = dstate.astype(jnp.bfloat16)
    dinput_far = jnp.einsum("hpn,hun->uhp", dstate_low, written, preferred_element_type=jnp.float32)
    per_head = jnp.einsum("hpn,uhp->uhn", dstate_low, inputs, preferred_element_type=jnp.float32)
    dwrite_far = jnp.sum(to_end.T[:, :, None] * per_head, axis=1)
    grad_inputs = (
        (dinput_local + dinput_far).astype(jnp.bfloat16).reshape(row_count, head_count * head_width)
    )
    grad_write, grad_read = side_by_side(
        (dwrite_local + dwrite_far, dread_local + dread_far), "head", 0, 1
    )
    return (mixer_out, grad_inputs, grad_write, grad_read)


def solution(mesh):
    return jax.shard_map(
        body,
        mesh=mesh,
        in_specs=(
            P("ctx", "head"),
            P("ctx", None),
            P("ctx", None),
            P("head", "ctx"),
            P(None, "head", "ctx"),
            P("ctx", "head"),
        ),
        out_specs=(
            P("ctx", "head"),
            P("ctx", "head"),
            P(("ctx", "head"), None),
            P(("ctx", "head"), None),
        ),
        check_vma=False,
    )
```

profile of v0, /device:TPU:1, one launch (start us, length us, event | category | flops | bytes accessed | tf_op | source)
XLA Modules:
  0.0 348.6 jit_solution(2481901428615450008)
XLA Ops:
  2.5 4.8 %collective-permute-start.1 = (f32[10]{0:T(128)S(1)}, f32[10]{0:T(128)S(1)}, u32[]{:S(2)}, u32[]{:S(2)}) collective-permute-start(f32[10]{0:T(128)S(1)} %slice_reduce_fusion.1), channel_id=1, source_target_pairs={{0,8},{8,0},{16,24},{24,16},{32,40},{40,32},{48,56},{56,48},{64,72... | collective-permute-start | bytes 128 | tf_op jit(solution)/shard_map/ppermute | solution.py:10
  8.7 5.8 %collective-permute-start.3 = (f32[10]{0:T(128)S(1)}, f32[10]{0:T(128)S(1)}, u32[]{:S(2)}, u32[]{:S(2)}) collective-permute-start(f32[10]{0:T(128)S(1)} %get-tuple-element.29), channel_id=1, source_target_pairs={{0,16},{8,24},{16,0},{24,8},{32,48},{40,56},{48,32},{56,40},{64,80... | collective-permute-start | bytes 128 | tf_op jit(solution)/shard_map/ppermute | solution.py:10
  14.5 0.9 collective-permute-done.3
  15.4 10.6 %collective-permute-start.5 = (f32[10]{0:T(128)S(1)}, f32[10]{0:T(128)S(1)}, u32[]{:S(2)}, u32[]{:S(2)}) collective-permute-start(f32[10]{0:T(128)S(1)} %get-tuple-element.27), channel_id=1, source_target_pairs={{0,32},{8,40},{16,48},{24,56},{32,0},{40,8},{48,16},{56,24},{64,96... | collective-permute-start | bytes 128 | tf_op jit(solution)/shard_map/ppermute | solution.py:10
  27.0 13.3 %collective-permute-start.7 = (f32[10]{0:T(128)S(1)}, f32[10]{0:T(128)S(1)}, u32[]{:S(2)}, u32[]{:S(2)}) collective-permute-start(f32[10]{0:T(128)S(1)} %get-tuple-element.25), channel_id=1, source_target_pairs={{0,64},{8,72},{16,80},{24,88},{32,96},{40,104},{48,112},{56,120},{... | collective-permute-start | bytes 128 | tf_op jit(solution)/shard_map/ppermute | solution.py:10
  41.2 3.2 collective-permute-start.9
  44.4 1.1 collective-permute-done.9
  45.6 4.2 %collective-permute-start.11 = (f32[10]{0:T(128)S(1)}, f32[10]{0:T(128)S(1)}, u32[]{:S(2)}, u32[]{:S(2)}) collective-permute-start(f32[10]{0:T(128)S(1)} %get-tuple-element.21), channel_id=1, source_target_pairs={{0,256},{8,264},{16,272},{24,280},{32,288},{40,296},{48,304},{56,3... | collective-permute-start | bytes 128 | tf_op jit(solution)/shard_map/ppermute | solution.py:10
  49.8 1.0 collective-permute-done.11
  51.7 7.6 %collective-permute-start.14 = (f32[10,64,128]{2,1,0:T(8,128)S(1)}, f32[10,64,128]{2,1,0:T(8,128)S(1)}, u32[]{:S(2)}, u32[]{:S(2)}) collective-permute-start(f32[10,64,128]{2,1,0:T(8,128)S(1)} %add_select_fusion.6), channel_id=1, source_target_pairs={{0,512},{8,520},{16,528},{24,536},{32,544},{40,552},{48,560},{56,5... | collective-permute-start | bytes 983048 | tf_op jit(solution)/shard_map/ppermute | solution.py:10
  59.3 1.9 collective-permute-start.13
  61.2 6.3 %collective-permute-done.13 = f32[10]{0:T(128)S(1)} collective-permute-done((f32[10]{0:T(128)S(1)}, f32[10]{0:T(128)S(1)}, u32[]{:S(2)}, u32[]{:S(2)}) %collective-permute-start.13) | collective-permute-done | bytes 72 | tf_op jit(solution)/shard_map/ppermute | solution.py:10
  67.8 3.9 %collective-permute-start.15 = (f32[10,64,128]{2,1,0:T(8,128)S(1)}, f32[10,64,128]{2,1,0:T(8,128)S(1)}, u32[]{:S(2)}, u32[]{:S(2)}) collective-permute-start(f32[10,64,128]{2,1,0:T(8,128)S(1)} %add_select_fusion.5), channel_id=1, source_target_pairs={{0,256},{8,264},{16,272},{24,280},{32,288},{40,296},{48,304},{56,3... | collective-permute-start | bytes 983048 | tf_op jit(solution)/shard_map/ppermute | solution.py:10
  72.0 11.6 %collective-permute-done.15 = f32[10,64,128]{2,1,0:T(8,128)S(1)} collective-permute-done((f32[10,64,128]{2,1,0:T(8,128)S(1)}, f32[10,64,128]{2,1,0:T(8,128)S(1)}, u32[]{:S(2)}, u32[]{:S(2)}) %collective-permute-start.15) | collective-permute-done | bytes 327712 | tf_op jit(solution)/shard_map/ppermute | solution.py:10
  83.8 2.1 collective-permute-start.16
  85.9 1.0 fusion.25
  87.1 1.3 convert_reduce_fusion
  88.4 6.9 %collective-permute-done.16 = f32[10,64,128]{2,1,0:T(8,128)} collective-permute-done((f32[10,64,128]{2,1,0:T(8,128)S(1)}, f32[10,64,128]{2,1,0:T(8,128)}, u32[]{:S(2)}, u32[]{:S(2)}) %collective-permute-start.16) | collective-permute-done | bytes 327712 | tf_op jit(solution)/shard_map/ppermute | solution.py:10
  95.3 1.1 fusion.38
  96.7 11.6 %collective-permute-start.17 = (f32[10,64,128]{2,1,0:T(8,128)S(1)}, f32[10,64,128]{2,1,0:T(8,128)S(1)}, u32[]{:S(2)}, u32[]{:S(2)}) collective-permute-start(f32[10,64,128]{2,1,0:T(8,128)S(1)} %add_select_fusion.3), channel_id=1, source_target_pairs={{0,64},{8,72},{16,80},{24,88},{32,96},{40,104},{48,112},{56,120},{... | collective-permute-start | bytes 983048 | tf_op jit(solution)/shard_map/ppermute | solution.py:10
  109.2 2.0 convolution_bitcast_fusion.1
  111.2 2.3 collective-permute-done.17
  113.8 21.7 %collective-permute-start.18 = (f32[10,64,128]{2,1,0:T(8,128)S(1)}, f32[10,64,128]{2,1,0:T(8,128)S(1)}, u32[]{:S(2)}, u32[]{:S(2)}) collective-permute-start(f32[10,64,128]{2,1,0:T(8,128)S(1)} %add_select_fusion.2), channel_id=1, source_target_pairs={{0,32},{8,40},{16,48},{24,56},{32,0},{40,8},{48,16},{56,24},{64,96... | collective-permute-start | bytes 983048 | tf_op jit(solution)/shard_map/ppermute | solution.py:10
  136.1 1.9 collective-permute-start
  138.1 29.0 %collective-permute-done.18 = f32[10,64,128]{2,1,0:T(8,128)S(1)} collective-permute-done((f32[10,64,128]{2,1,0:T(8,128)S(1)}, f32[10,64,128]{2,1,0:T(8,128)S(1)}, u32[]{:S(2)}, u32[]{:S(2)}) %collective-permute-start.18) | collective-permute-done | bytes 327712 | tf_op jit(solution)/shard_map/ppermute | solution.py:10
  167.6 1.9 collective-permute-start.19
  169.7 6.0 %collective-permute-start.2 = (f32[10,64,128]{2,1,0:T(8,128)S(1)}, f32[10,64,128]{2,1,0:T(8,128)S(1)}, u32[]{:S(2)}, u32[]{:S(2)}) collective-permute-start(f32[10,64,128]{2,1,0:T(8,128)S(1)} %add_select_fusion.12), channel_id=1, source_target_pairs={{0,16},{8,24},{16,0},{24,8},{32,48},{40,56},{48,32},{56,40},{64,80... | collective-permute-start | bytes 983048 | tf_op jit(solution)/shard_map/ppermute | solution.py:10
  176.2 17.4 %collective-permute-done.19 = f32[10,64,128]{2,1,0:T(8,128)S(1)} collective-permute-done((f32[10,64,128]{2,1,0:T(8,128)S(1)}, f32[10,64,128]{2,1,0:T(8,128)S(1)}, u32[]{:S(2)}, u32[]{:S(2)}) %collective-permute-start.19) | collective-permute-done | bytes 327712 | tf_op jit(solution)/shard_map/ppermute | solution.py:10
  193.8 1.9 collective-permute-start.20
  195.7 4.9 %collective-permute-done.2 = f32[10,64,128]{2,1,0:T(8,128)S(1)} collective-permute-done((f32[10,64,128]{2,1,0:T(8,128)S(1)}, f32[10,64,128]{2,1,0:T(8,128)S(1)}, u32[]{:S(2)}, u32[]{:S(2)}) %collective-permute-start.2) | collective-permute-done | bytes 327712 | tf_op jit(solution)/shard_map/ppermute | solution.py:10
  200.6 1.1 convolution_bitcast_fusion.11
  202.1 6.0 %collective-permute-done.20 = f32[10,64,128]{2,1,0:T(8,128)S(1)} collective-permute-done((f32[10,64,128]{2,1,0:T(8,128)S(1)}, f32[10,64,128]{2,1,0:T(8,128)S(1)}, u32[]{:S(2)}, u32[]{:S(2)}) %collective-permute-start.20) | collective-permute-done | bytes 327712 | tf_op jit(solution)/shard_map/ppermute | solution.py:10
  208.3 1.9 collective-permute-start.4
  212.4 29.7 %collective-permute-done.4 = f32[10,64,128]{2,1,0:T(8,128)S(1)} collective-permute-done((f32[10,64,128]{2,1,0:T(8,128)S(1)}, f32[10,64,128]{2,1,0:T(8,128)S(1)}, u32[]{:S(2)}, u32[]{:S(2)}) %collective-permute-start.4) | collective-permute-done | bytes 327712 | tf_op jit(solution)/shard_map/ppermute | solution.py:10
  242.3 18.1 %collective-permute-start.6 = (f32[10,64,128]{2,1,0:T(8,128)S(1)}, f32[10,64,128]{2,1,0:T(8,128)S(1)}, u32[]{:S(2)}, u32[]{:S(2)}) collective-permute-start(f32[10,64,128]{2,1,0:T(8,128)S(1)} %add_select_fusion.10), channel_id=1, source_target_pairs={{0,64},{8,72},{16,80},{24,88},{32,96},{40,104},{48,112},{56,120},{... | collective-permute-start | bytes 983048 | tf_op jit(solution)/shard_map/ppermute | solution.py:10
  261.3 18.7 %collective-permute-done.6 = f32[10,64,128]{2,1,0:T(8,128)S(1)} collective-permute-done((f32[10,64,128]{2,1,0:T(8,128)S(1)}, f32[10,64,128]{2,1,0:T(8,128)S(1)}, u32[]{:S(2)}, u32[]{:S(2)}) %collective-permute-start.6) | collective-permute-done | bytes 327712 | tf_op jit(solution)/shard_map/ppermute | solution.py:10
  280.1 1.9 collective-permute-start.8
  283.0 7.8 %collective-permute-done.8 = f32[10,64,128]{2,1,0:T(8,128)S(1)} collective-permute-done((f32[10,64,128]{2,1,0:T(8,128)S(1)}, f32[10,64,128]{2,1,0:T(8,128)S(1)}, u32[]{:S(2)}, u32[]{:S(2)}) %collective-permute-start.8) | collective-permute-done | bytes 327712 | tf_op jit(solution)/shard_map/ppermute | solution.py:10
  290.9 2.1 collective-permute-start.10
  293.5 1.3 fusion.4
  294.8 15.5 %collective-permute-done.10 = f32[10,64,128]{2,1,0:T(8,128)S(1)} collective-permute-done((f32[10,64,128]{2,1,0:T(8,128)S(1)}, f32[10,64,128]{2,1,0:T(8,128)S(1)}, u32[]{:S(2)}, u32[]{:S(2)}) %collective-permute-start.10) | collective-permute-done | bytes 327712 | tf_op jit(solution)/shard_map/ppermute | solution.py:10
  310.5 4.7 %collective-permute-start.12 = (f32[10,64,128]{2,1,0:T(8,128)S(1)}, f32[10,64,128]{2,1,0:T(8,128)S(1)}, u32[]{:S(2)}, u32[]{:S(2)}) collective-permute-start(f32[10,64,128]{2,1,0:T(8,128)S(1)} %add_select_fusion.7), channel_id=1, source_target_pairs={{0,512},{8,520},{16,528},{24,536},{32,544},{40,552},{48,560},{56,5... | collective-permute-start | bytes 983048 | tf_op jit(solution)/shard_map/ppermute | solution.py:10
  316.2 16.5 %collective-permute-done.12 = f32[10,64,128]{2,1,0:T(8,128)S(1)} collective-permute-done((f32[10,64,128]{2,1,0:T(8,128)S(1)}, f32[10,64,128]{2,1,0:T(8,128)S(1)}, u32[]{:S(2)}, u32[]{:S(2)}) %collective-permute-start.12) | collective-permute-done | bytes 327712 | tf_op jit(solution)/shard_map/ppermute | solution.py:10
  334.1 1.9 copy.29
  336.0 4.4 %all-to-all-start = ((f32[8,32,256]{2,1,0:T(8,128)}), f32[8,32,256]{2,1,0:T(8,128)}, u32[]{:S(2)}, u32[]{:S(2)}) async-start(f32[8,32,256]{2,1,0:T(8,128)} %bitcast.242), calls=%async_computation | async-start | bytes 524288 | tf_op jit(solution)/shard_map/all_to_all | solution.py:21
  341.5 1.7 fusion.16
  344.1 2.9 all-to-all-done
  347.0 1.0 reduce_sum.33
  (134 shorter events, 20.5 us)
Async XLA Ops:
  0.6 50.8 %copy-start = (bf16[256,128]{1,0:T(8,128)(2,1)S(1)}, bf16[256,128]{1,0:T(8,128)(2,1)}, u32[]{:S(2)}) copy-start(bf16[256,128]{1,0:T(8,128)(2,1)} %param.8) | copy-start | bytes 196612
  2.5 6.1 %collective-permute-start.1 = (f32[10]{0:T(128)S(1)}, f32[10]{0:T(128)S(1)}, u32[]{:S(2)}, u32[]{:S(2)}) collective-permute-start(f32[10]{0:T(128)S(1)} %slice_reduce_fusion.1), channel_id=1, source_target_pairs={{0,8},{8,0},{16,24},{24,16},{32,40},{40,32},{48,56},{56,48},{64,72... | collective-permute-start | bytes 128 | tf_op jit(solution)/shard_map/ppermute | solution.py:10
  8.6 158.7 %copy-start.29 = (f32[10]{0:T(128)}, f32[10]{0:T(128)S(1)}, u32[]{:S(2)}) copy-start(f32[10]{0:T(128)S(1)} %get-tuple-element.28) | copy-start | bytes 124
  8.7 160.9 %copy-start.23 = (f32[10]{0:T(128)}, f32[10]{0:T(128)S(1)}, u32[]{:S(2)}) copy-start(f32[10]{0:T(128)S(1)} %get-tuple-element.53) | copy-start | bytes 124
  8.7 6.8 %collective-permute-start.3 = (f32[10]{0:T(128)S(1)}, f32[10]{0:T(128)S(1)}, u32[]{:S(2)}, u32[]{:S(2)}) collective-permute-start(f32[10]{0:T(128)S(1)} %get-tuple-element.29), channel_id=1, source_target_pairs={{0,16},{8,24},{16,0},{24,8},{32,48},{40,56},{48,32},{56,40},{64,80... | collective-permute-start | bytes 128 | tf_op jit(solution)/shard_map/ppermute | solution.py:10
  15.4 98.1 %copy-start.27 = (f32[10]{0:T(128)}, f32[10]{0:T(128)S(1)}, u32[]{:S(2)}) copy-start(f32[10]{0:T(128)S(1)} %get-tuple-element.26) | copy-start | bytes 124
  15.4 11.6 %collective-permute-start.5 = (f32[10]{0:T(128)S(1)}, f32[10]{0:T(128)S(1)}, u32[]{:S(2)}, u32[]{:S(2)}) collective-permute-start(f32[10]{0:T(128)S(1)} %get-tuple-element.27), channel_id=1, source_target_pairs={{0,32},{8,40},{16,48},{24,56},{32,0},{40,8},{48,16},{56,24},{64,96... | collective-permute-start | bytes 128 | tf_op jit(solution)/shard_map/ppermute | solution.py:10
  27.0 69.4 %copy-start.19 = (f32[10]{0:T(128)}, f32[10]{0:T(128)S(1)}, u32[]{:S(2)}) copy-start(f32[10]{0:T(128)S(1)} %get-tuple-element.24) | copy-start | bytes 124
  27.0 14.2 %collective-permute-start.7 = (f32[10]{0:T(128)S(1)}, f32[10]{0:T(128)S(1)}, u32[]{:S(2)}, u32[]{:S(2)}) collective-permute-start(f32[10]{0:T(128)S(1)} %get-tuple-element.25), channel_id=1, source_target_pairs={{0,64},{8,72},{16,80},{24,88},{32,96},{40,104},{48,112},{56,120},{... | collective-permute-start | bytes 128 | tf_op jit(solution)/shard_map/ppermute | solution.py:10
  41.2 42.3 %copy-start.17 = (f32[10]{0:T(128)}, f32[10]{0:T(128)S(1)}, u32[]{:S(2)}) copy-start(f32[10]{0:T(128)S(1)} %get-tuple-element.22) | copy-start | bytes 124
  41.2 4.3 %collective-permute-start.9 = (f32[10]{0:T(128)S(1)}, f32[10]{0:T(128)S(1)}, u32[]{:S(2)}, u32[]{:S(2)}) collective-permute-start(f32[10]{0:T(128)S(1)} %get-tuple-element.23), channel_id=1, source_target_pairs={{0,128},{8,136},{16,144},{24,152},{32,160},{40,168},{48,176},{56,1... | collective-permute-start | bytes 128 | tf_op jit(solution)/shard_map/ppermute | solution.py:10
  45.6 22.2 %copy-start.25 = (f32[10]{0:T(128)}, f32[10]{0:T(128)S(1)}, u32[]{:S(2)}) copy-start(f32[10]{0:T(128)S(1)} %get-tuple-element.20) | copy-start | bytes 124
  45.6 5.2 %collective-permute-start.11 = (f32[10]{0:T(128)S(1)}, f32[10]{0:T(128)S(1)}, u32[]{:S(2)}, u32[]{:S(2)}) collective-permute-start(f32[10]{0:T(128)S(1)} %get-tuple-element.21), channel_id=1, source_target_pairs={{0,256},{8,264},{16,272},{24,280},{32,288},{40,296},{48,304},{56,3... | collective-permute-start | bytes 128 | tf_op jit(solution)/shard_map/ppermute | solution.py:10
  51.3 44.0 %copy-start.11 = (f32[10]{0:T(128)}, f32[10]{0:T(128)S(1)}, u32[]{:S(2)}) copy-start(f32[10]{0:T(128)S(1)} %get-tuple-element.52) | copy-start | bytes 124
  51.3 44.0 %copy-start.21 = (f32[10]{0:T(128)}, f32[10]{0:T(128)S(1)}, u32[]{:S(2)}) copy-start(f32[10]{0:T(128)S(1)} %get-tuple-element.51) | copy-start | bytes 124
  51.3 115.9 %copy-start.13 = (f32[10]{0:T(128)}, f32[10]{0:T(128)S(1)}, u32[]{:S(2)}) copy-start(f32[10]{0:T(128)S(1)} %get-tuple-element.50) | copy-start | bytes 124
  51.3 115.9 %copy-start.15 = (f32[10]{0:T(128)}, f32[10]{0:T(128)S(1)}, u32[]{:S(2)}) copy-start(f32[10]{0:T(128)S(1)} %get-tuple-element.49) | copy-start | bytes 124
  51.3 118.2 %copy-start.31 = (f32[10]{0:T(128)}, f32[10]{0:T(128)S(1)}, u32[]{:S(2)}) copy-start(f32[10]{0:T(128)S(1)} %get-tuple-element.47) | copy-start | bytes 124
  51.7 20.1 %copy-start.4 = (bf16[256,128]{1,0:T(8,128)(2,1)S(1)}, bf16[256,128]{1,0:T(8,128)(2,1)}, u32[]{:S(2)}) copy-start(bf16[256,128]{1,0:T(8,128)(2,1)} %param.7) | copy-start | bytes 196612
  51.7 15.8 %collective-permute-start.14 = (f32[10,64,128]{2,1,0:T(8,128)S(1)}, f32[10,64,128]{2,1,0:T(8,128)S(1)}, u32[]{:S(2)}, u32[]{:S(2)}) collective-permute-start(f32[10,64,128]{2,1,0:T(8,128)S(1)} %add_select_fusion.6), channel_id=1, source_target_pairs={{0,512},{8,520},{16,528},{24,536},{32,544},{40,552},{48,560},{56,5... | collective-permute-start | bytes 983048 | tf_op jit(solution)/shard_map/ppermute | solution.py:10
  59.3 8.2 %collective-permute-start.13 = (f32[10]{0:T(128)S(1)}, f32[10]{0:T(128)S(1)}, u32[]{:S(2)}, u32[]{:S(2)}) collective-permute-start(f32[10]{0:T(128)S(1)} %get-tuple-element.13), channel_id=1, source_target_pairs={{0,512},{8,520},{16,528},{24,536},{32,544},{40,552},{48,560},{56,5... | collective-permute-start | bytes 128 | tf_op jit(solution)/shard_map/ppermute | solution.py:10
  67.8 15.8 %collective-permute-start.15 = (f32[10,64,128]{2,1,0:T(8,128)S(1)}, f32[10,64,128]{2,1,0:T(8,128)S(1)}, u32[]{:S(2)}, u32[]{:S(2)}) collective-permute-start(f32[10,64,128]{2,1,0:T(8,128)S(1)} %add_select_fusion.5), channel_id=1, source_target_pairs={{0,256},{8,264},{16,272},{24,280},{32,288},{40,296},{48,304},{56,3... | collective-permute-start | bytes 983048 | tf_op jit(solution)/shard_map/ppermute | solution.py:10
  83.8 11.5 %collective-permute-start.16 = (f32[10,64,128]{2,1,0:T(8,128)S(1)}, f32[10,64,128]{2,1,0:T(8,128)}, u32[]{:S(2)}, u32[]{:S(2)}) collective-permute-start(f32[10,64,128]{2,1,0:T(8,128)S(1)} %add_select_fusion.4), channel_id=1, source_target_pairs={{0,128},{8,136},{16,144},{24,152},{32,160},{40,168},{48,176},{56,1... | collective-permute-start | bytes 983048 | tf_op jit(solution)/shard_map/ppermute | solution.py:10
  87.1 48.5 %copy-start.9 = (bf16[256,640]{0,1:T(8,128)(2,1)}, bf16[256,640]{0,1:T(8,128)(2,1)S(1)}, u32[]{:S(2)}) copy-start(bf16[256,640]{0,1:T(8,128)(2,1)S(1)} %copy.27) | copy-start | bytes 983044
  96.7 16.8 %collective-permute-start.17 = (f32[10,64,128]{2,1,0:T(8,128)S(1)}, f32[10,64,128]{2,1,0:T(8,128)S(1)}, u32[]{:S(2)}, u32[]{:S(2)}) collective-permute-start(f32[10,64,128]{2,1,0:T(8,128)S(1)} %add_select_fusion.3), channel_id=1, source_target_pairs={{0,64},{8,72},{16,80},{24,88},{32,96},{40,104},{48,112},{56,120},{... | collective-permute-start | bytes 983048 | tf_op jit(solution)/shard_map/ppermute | solution.py:10
  113.8 53.3 %collective-permute-start.18 = (f32[10,64,128]{2,1,0:T(8,128)S(1)}, f32[10,64,128]{2,1,0:T(8,128)S(1)}, u32[]{:S(2)}, u32[]{:S(2)}) collective-permute-start(f32[10,64,128]{2,1,0:T(8,128)S(1)} %add_select_fusion.2), channel_id=1, source_target_pairs={{0,32},{8,40},{16,48},{24,56},{32,0},{40,8},{48,16},{56,24},{64,96... | collective-permute-start | bytes 983048 | tf_op jit(solution)/shard_map/ppermute | solution.py:10
  136.1 33.4 %collective-permute-start = (f32[10,64,128]{2,1,0:T(8,128)S(1)}, f32[10,64,128]{2,1,0:T(8,128)S(1)}, u32[]{:S(2)}, u32[]{:S(2)}) collective-permute-start(f32[10,64,128]{2,1,0:T(8,128)S(1)} %convolution_bitcast_fusion.9), channel_id=1, source_target_pairs={{0,8},{8,0},{16,24},{24,16},{32,40},{40,32},{48,56},{56,48},{64,72... | collective-permute-start | bytes 983048 | tf_op jit(solution)/shard_map/ppermute | solution.py:10
  167.6 25.9 %collective-permute-start.19 = (f32[10,64,128]{2,1,0:T(8,128)S(1)}, f32[10,64,128]{2,1,0:T(8,128)S(1)}, u32[]{:S(2)}, u32[]{:S(2)}) collective-permute-start(f32[10,64,128]{2,1,0:T(8,128)S(1)} %add_select_fusion.1), channel_id=1, source_target_pairs={{0,16},{8,24},{16,0},{24,8},{32,48},{40,56},{48,32},{56,40},{64,80... | collective-permute-start | bytes 983048 | tf_op jit(solution)/shard_map/ppermute | solution.py:10
  169.6 24.0 %copy-start.33 = (f32[10]{0:T(128)S(1)}, f32[10]{0:T(128)}, u32[]{:S(2)}) copy-start(f32[10]{0:T(128)} %get-tuple-element.48) | copy-start | bytes 124
  169.7 23.8 %copy-start.24 = (f32[10]{0:T(128)S(1)}, f32[10]{0:T(128)}, u32[]{:S(2)}) copy-start(f32[10]{0:T(128)} %copy-done.23) | copy-start | bytes 124
  169.7 30.9 %collective-permute-start.2 = (f32[10,64,128]{2,1,0:T(8,128)S(1)}, f32[10,64,128]{2,1,0:T(8,128)S(1)}, u32[]{:S(2)}, u32[]{:S(2)}) collective-permute-start(f32[10,64,128]{2,1,0:T(8,128)S(1)} %add_select_fusion.12), channel_id=1, source_target_pairs={{0,16},{8,24},{16,0},{24,8},{32,48},{40,56},{48,32},{56,40},{64,80... | collective-permute-start | bytes 983048 | tf_op jit(solution)/shard_map/ppermute | solution.py:10
  193.8 14.3 %collective-permute-start.20 = (f32[10,64,128]{2,1,0:T(8,128)S(1)}, f32[10,64,128]{2,1,0:T(8,128)S(1)}, u32[]{:S(2)}, u32[]{:S(2)}) collective-permute-start(f32[10,64,128]{2,1,0:T(8,128)S(1)} %add_select_fusion), channel_id=1, source_target_pairs={{0,8},{8,0},{16,24},{24,16},{32,40},{40,32},{48,56},{56,48},{64,72... | collective-permute-start | bytes 983048 | tf_op jit(solution)/shard_map/ppermute | solution.py:10
  208.3 33.8 %collective-permute-start.4 = (f32[10,64,128]{2,1,0:T(8,128)S(1)}, f32[10,64,128]{2,1,0:T(8,128)S(1)}, u32[]{:S(2)}, u32[]{:S(2)}) collective-permute-start(f32[10,64,128]{2,1,0:T(8,128)S(1)} %get-tuple-element.40), channel_id=1, source_target_pairs={{0,32},{8,40},{16,48},{24,56},{32,0},{40,8},{48,16},{56,24},{64,96... | collective-permute-start | bytes 983048 | tf_op jit(solution)/shard_map/ppermute | solution.py:10
  211.8 30.3 %copy-start.16 = (f32[10]{0:T(128)S(1)}, f32[10]{0:T(128)}, u32[]{:S(2)}) copy-start(f32[10]{0:T(128)} %copy-done.15) | copy-start | bytes 124
  211.8 30.3 %copy-start.28 = (f32[10]{0:T(128)S(1)}, f32[10]{0:T(128)}, u32[]{:S(2)}) copy-start(f32[10]{0:T(128)} %copy-done.27) | copy-start | bytes 124
  242.3 37.7 %collective-permute-start.6 = (f32[10,64,128]{2,1,0:T(8,128)S(1)}, f32[10,64,128]{2,1,0:T(8,128)S(1)}, u32[]{:S(2)}, u32[]{:S(2)}) collective-permute-start(f32[10,64,128]{2,1,0:T(8,128)S(1)} %add_select_fusion.10), channel_id=1, source_target_pairs={{0,64},{8,72},{16,80},{24,88},{32,96},{40,104},{48,112},{56,120},{... | collective-permute-start | bytes 983048 | tf_op jit(solution)/shard_map/ppermute | solution.py:10
  260.8 19.2 %copy-start.14 = (f32[10]{0:T(128)S(1)}, f32[10]{0:T(128)}, u32[]{:S(2)}) copy-start(f32[10]{0:T(128)} %copy-done.13) | copy-start | bytes 124
  260.8 19.2 %copy-start.20 = (f32[10]{0:T(128)S(1)}, f32[10]{0:T(128)}, u32[]{:S(2)}) copy-start(f32[10]{0:T(128)} %copy-done.19) | copy-start | bytes 124
  280.1 10.7 %collective-permute-start.8 = (f32[10,64,128]{2,1,0:T(8,128)S(1)}, f32[10,64,128]{2,1,0:T(8,128)S(1)}, u32[]{:S(2)}, u32[]{:S(2)}) collective-permute-start(f32[10,64,128]{2,1,0:T(8,128)S(1)} %add_select_fusion.9), channel_id=1, source_target_pairs={{0,128},{8,136},{16,144},{24,152},{32,160},{40,168},{48,176},{56,1... | collective-permute-start | bytes 983048 | tf_op jit(solution)/shard_map/ppermute | solution.py:10
  282.5 8.3 %copy-start.18 = (f32[10]{0:T(128)S(1)}, f32[10]{0:T(128)}, u32[]{:S(2)}) copy-start(f32[10]{0:T(128)} %copy-done.17) | copy-start | bytes 124
  282.5 8.3 %copy-start.22 = (f32[10]{0:T(128)S(1)}, f32[10]{0:T(128)}, u32[]{:S(2)}) copy-start(f32[10]{0:T(128)} %copy-done.21) | copy-start | bytes 124
  290.9 19.4 %collective-permute-start.10 = (f32[10,64,128]{2,1,0:T(8,128)S(1)}, f32[10,64,128]{2,1,0:T(8,128)S(1)}, u32[]{:S(2)}, u32[]{:S(2)}) collective-permute-start(f32[10,64,128]{2,1,0:T(8,128)S(1)} %add_select_fusion.8), channel_id=1, source_target_pairs={{0,256},{8,264},{16,272},{24,280},{32,288},{40,296},{48,304},{56,3... | collective-permute-start | bytes 983048 | tf_op jit(solution)/shard_map/ppermute | solution.py:10
  293.5 16.9 %copy-start.12 = (f32[10]{0:T(128)S(1)}, f32[10]{0:T(128)}, u32[]{:S(2)}) copy-start(f32[10]{0:T(128)} %copy-done.11) | copy-start | bytes 124
  293.5 16.8 %copy-start.26 = (f32[10]{0:T(128)S(1)}, f32[10]{0:T(128)}, u32[]{:S(2)}) copy-start(f32[10]{0:T(128)} %copy-done.25) | copy-start | bytes 124
  310.5 22.2 %collective-permute-start.12 = (f32[10,64,128]{2,1,0:T(8,128)S(1)}, f32[10,64,128]{2,1,0:T(8,128)S(1)}, u32[]{:S(2)}, u32[]{:S(2)}) collective-permute-start(f32[10,64,128]{2,1,0:T(8,128)S(1)} %add_select_fusion.7), channel_id=1, source_target_pairs={{0,512},{8,520},{16,528},{24,536},{32,544},{40,552},{48,560},{56,5... | collective-permute-start | bytes 983048 | tf_op jit(solution)/shard_map/ppermute | solution.py:10
  315.7 17.0 %copy-start.5 = (f32[256,128]{0,1:T(8,128)S(1)}, f32[256,128]{0,1:T(8,128)}, u32[]{:S(2)}) copy-start(f32[256,128]{0,1:T(8,128)} %convolution_bitcast_fusion.11) | copy-start | bytes 393220
  315.7 17.0 %copy-start.6 = (f32[256,128]{0,1:T(8,128)S(1)}, f32[256,128]{0,1:T(8,128)}, u32[]{:S(2)}) copy-start(f32[256,128]{0,1:T(8,128)} %fusion.135) | copy-start | bytes 393220
  336.0 11.0 %all-to-all-start = ((f32[8,32,256]{2,1,0:T(8,128)}), f32[8,32,256]{2,1,0:T(8,128)}, u32[]{:S(2)}, u32[]{:S(2)}) async-start(f32[8,32,256]{2,1,0:T(8,128)} %bitcast.242), calls=%async_computation | async-start | bytes 524288 | tf_op jit(solution)/shard_map/all_to_all | solution.py:21
  (8 other events, 32.7 us)
where the time goes:
time: 350 us; the launch traced here: 349 us
  waiting for transfers between devices  180 us (51%)
  starting transfers between devices  136 us (39%)
  matrix products  17.9 us (5%)
  local copies, waits for them, and re-layouts  6.86 us (2%)
  other arithmetic  6.18 us (2%)
    ppermute x21, waiting for transfers between devices, from_partner(): return lax.ppermute(value, axis, pairs)  178 us
    ppermute x21, starting transfers between devices, from_partner(): return lax.ppermute(value, axis, pairs)  131 us
  transfers between devices with their start and end apart: 22, of which 19 were waited for; matrix products, arithmetic and copies ran while one was open for 6% of the time, Pallas kernels for 0%

commit v1 on v0

v1 whole, which is shorter than its diff:
```python
import jax
import jax.numpy as jnp
from jax import lax
from jax.sharding import PartitionSpec as P


def exchange(value, bit):
    pairs = [(source, source ^ 2**bit) for source in range(lax.axis_size("ctx"))]
    return lax.ppermute(value, "ctx", pairs)


def to_left(value):
    pairs = [(source, source - 1) for source in range(1, lax.axis_size("ctx"), 2)]
    return lax.ppermute(value, "ctx", pairs)


def sum_at_owner(value, axis):
    pieces = value.reshape(lax.axis_size(axis), -1, value.shape[1])
    return lax.all_to_all(pieces, axis, split_axis=0, concat_axis=0, tiled=True).sum(axis=0)


def block_spans(total, shard_index, level_count):
    size = 2**level_count
    mine = jnp.broadcast_to(total[None, None, :], (size, 1, total.shape[0]))
    spans = lax.all_to_all(mine, "ctx", split_axis=0, concat_axis=0, tiled=True)
    spans = spans[:, 0]
    stretch = jnp.arange(size)[:, None]
    own_spans, peer_spans, offsets = ([], [], [])
    offset = jnp.zeros_like(total)
    for bit in range(level_count):
        block = shard_index // 2**bit
        own = jnp.sum(jnp.where(stretch // 2**bit == block, spans, 0.0), axis=0)
        peer = jnp.sum(jnp.where(stretch // 2**bit == (block ^ 1), spans, 0.0), axis=0)
        own_spans.append(own)
        peer_spans.append(peer)
        offsets.append(offset)
        offset = offset + jnp.where(block % 2 == 1, peer, 0.0)
    return own_spans, peer_spans, offsets


Z_BITS = 4


class Side:
    def __init__(self, keep, pull, shard_index):
        keep, pull, shard_index = lax.optimization_barrier((keep, pull, shard_index))
        self.given = (keep, pull, shard_index)
        self.keep, self.pull = (
            [factor[:, None, None] for factor in factors] for factors in (keep, pull)
        )
        self.place = shard_index % 2

    def join(self, bit, block, peer):
        return self.keep[bit] * block + self.pull[bit] * peer


class Up(Side):
    def part(self, value, place):
        half = value.shape[0] // 2
        return lax.dynamic_slice_in_dim(value, place * half, half, axis=0)

    def mine(self, value):
        return self.part(value, self.place)

    def join_half(self, bit, block, peer):
        return self.mine(self.keep[bit]) * block + self.mine(self.pull[bit]) * peer

    def whole(self, own_half, other_half):
        ring = jnp.concatenate([own_half, other_half, own_half], axis=0)
        half = own_half.shape[0]
        return lax.dynamic_slice_in_dim(ring, self.place * half, 2 * half, axis=0)


class Down(Side):
    def mine(self, value):
        half = value.shape[1] // 2
        return jnp.where(self.place == 1, value[:, half:], value[:, :half])

    def theirs(self, value):
        half = value.shape[1] // 2
        return jnp.where(self.place == 1, value[:, :half], value[:, half:])

    def whole(self, own_half, other_half):
        ahead = jnp.concatenate([own_half, other_half], axis=1)
        behind = jnp.concatenate([other_half, own_half], axis=1)
        return jnp.where(self.place == 1, behind, ahead)


def mixer(seq_inputs, state_write, state_read, log_decay, level_weight, grad_out):
    row_count = seq_inputs.shape[0]
    head_count = log_decay.shape[0]
    head_width = seq_inputs.shape[1] // head_count
    inputs = seq_inputs.reshape(row_count, head_count, head_width)
    cotangent = grad_out.reshape(row_count, head_count, head_width)
    scaled = level_weight.astype(jnp.float32) * 0.125
    running = jnp.cumsum(log_decay, axis=1)
    total = running[:, -1]
    shard_index = lax.axis_index("ctx")
    level_count = lax.axis_size("ctx").bit_length() - 1
    own_spans, peer_spans, offsets = block_spans(total, shard_index, level_count)
    is_right = [shard_index // 2**bit % 2 == 1 for bit in range(level_count)]
    keep = [
        jnp.where(is_right[bit], 1.0, jnp.exp(peer_spans[bit])) for bit in range(level_count)
    ]
    pull = [jnp.where(is_right[bit], jnp.exp(own_spans[bit]), 1.0) for bit in range(level_count)]
    up = Up(keep, pull, shard_index)
    down = Down(*up.given)

    to_end = jnp.exp(total[:, None] - running)
    written = (to_end[:, :, None] * state_write.astype(jnp.float32)[None]).astype(jnp.bfloat16)
    state = jnp.einsum("uhp,hun->hpn", inputs, written, preferred_element_type=jnp.float32)
    coefficients, weighted, level_grads = ([], [], [])
    for bit in range(level_count):
        coeff = jnp.where(
            is_right[bit], scaled[bit + 1] * jnp.exp(running + offsets[bit][:, None]), 0.0
        )
        coefficients.append(coeff.T[:, :, None])
        weighted.append((coefficients[bit] * cotangent.astype(jnp.float32)).astype(jnp.bfloat16))
        level_grads.append(
            jnp.einsum("thp,tn->hpn", weighted[bit], state_read, preferred_element_type=jnp.float32)
        )
    buckets = [exchange(state, 0)]
    pair_state = up.join(0, state, buckets[0])
    half_state = up.mine(pair_state)
    half_buckets = []
    for bit in range(1, Z_BITS):
        half_buckets.append(exchange(half_state, bit))
        half_state = up.join_half(bit, half_state, half_buckets[-1])
    early = exchange(jnp.stack(half_buckets[:-1]), 0)
    late = exchange(half_buckets[-1], 0)
    block_state = pair_state
    for bit in range(1, Z_BITS):
        other_half = late if bit == Z_BITS - 1 else early[bit - 1]
        buckets.append(up.whole(half_buckets[bit - 1], other_half))
        block_state = up.join(bit, block_state, buckets[bit])
    for bit in range(Z_BITS, level_count):
        buckets.append(exchange(block_state, bit))
        if bit + 1 < level_count:
            block_state = up.join(bit, block_state, buckets[bit])
    carried = jnp.zeros_like(state)

    def step_down(bit, carried, level_grad):
        incoming = exchange(down.pull[bit] * carried + level_grad, bit)
        return down.keep[bit] * carried + incoming

    first_grads = to_left(level_grads[0])
    half_grads = exchange(jnp.stack([down.theirs(level_grads[bit]) for bit in range(1, Z_BITS)]), 0)
    for bit in reversed(range(Z_BITS, level_count)):
        carried = step_down(bit, carried, level_grads[bit])
    half_carried = down.mine(carried) + exchange(down.theirs(carried), 0)
    for bit in reversed(range(1, Z_BITS)):
        half_grad = down.mine(level_grads[bit]) + half_grads[bit - 1]
        half_carried = step_down(bit, half_carried, half_grad)
    pair_grad = down.whole(half_carried, exchange(half_carried, 0))
    dstate = down.keep[0] * pair_grad + first_grads
    scores = jnp.dot(state_read, state_write.T, preferred_element_type=jnp.float32)
    token_positions = jnp.arange(row_count)
    causal = (token_positions[:, None] >= token_positions[None, :])[None]
    gaps = running[:, :, None] - running[:, None, :]
    local_weight = (
        jnp.where(causal, jnp.exp(jnp.where(causal, gaps, 0.0)), 0.0) * scaled[0][:, :, None]
    )
    mixing = (local_weight * scores[None]).astype(jnp.bfloat16)
    y_local = jnp.einsum("htu,uhp->thp", mixing, inputs, preferred_element_type=jnp.float32)
    d_mixing = jnp.einsum("thp,uhp->htu", cotangent, inputs, preferred_element_type=jnp.float32)
    d_scores = (d_mixing * local_weight).astype(jnp.bfloat16)
    dread_local = jnp.einsum("htu,un->tn", d_scores, state_write, preferred_element_type=jnp.float32)
    dwrite_local = jnp.einsum("htu,tn->un", d_scores, state_read, preferred_element_type=jnp.float32)
    dinput_local = jnp.einsum("htu,thp->uhp", mixing, cotangent, preferred_element_type=jnp.float32)
    read_wide = state_read.astype(jnp.float32)
    y_far = jnp.zeros((row_count, head_count, head_width), jnp.float32)
    dread_far = jnp.zeros((row_count, state_read.shape[1]), jnp.float32)
    for bit in range(level_count):
        raw = jnp.einsum("tn,hpn->thp", read_wide, buckets[bit], precision=lax.Precision.HIGHEST)
        y_far = y_far + raw * coefficients[bit]
        dread_far = dread_far + jnp.einsum(
            "thp,hpn->tn",
            weighted[bit].astype(jnp.float32),
            buckets[bit],
            precision=lax.Precision.HIGHEST,
        )
    mixer_out = (y_local + y_far).astype(jnp.bfloat16).reshape(row_count, head_count * head_width)
    dstate_low = dstate.astype(jnp.bfloat16)
    dinput_far = jnp.einsum("hpn,hun->uhp", dstate_low, written, preferred_element_type=jnp.float32)
    per_head = jnp.einsum("hpn,uhp->uhn", dstate_low, inputs, preferred_element_type=jnp.float32)
    dwrite_far = jnp.sum(to_end.T[:, :, None] * per_head, axis=1)
    grad_inputs = (
        (dinput_local + dinput_far).astype(jnp.bfloat16).reshape(row_count, head_count * head_width)
    )
    grad_read = sum_at_owner(dread_local + dread_far, "head")
    grad_write = sum_at_owner(dwrite_local + dwrite_far, "head")
    return (mixer_out, grad_inputs, grad_write, grad_read)


def solution(mesh):
    return jax.shard_map(
        mixer,
        mesh=mesh,
        in_specs=(
            P("ctx", "head"),
            P("ctx", None),
            P("ctx", None),
            P("head", "ctx"),
            P(None, "head", "ctx"),
            P("ctx", "head"),
        ),
        out_specs=(
            P("ctx", "head"),
            P("ctx", "head"),
            P(("ctx", "head"), None),
            P(("ctx", "head"), None),
        ),
        check_vma=False,
    )
```

time: 350 us -> 218 us (0.62)
  waiting for transfers between devices: 180 us -> 47.2 us
  matrix products: 17.9 us -> 23.2 us
  starting transfers between devices: 136 us -> 132 us
    ppermute x21 -> x19, waiting for transfers between devices: 178 us -> 39.7 us  [the longest x18 39.7 us: exchange(): return lax.ppermute(value, 'ctx', pairs)]
    ppermute x21 -> x19, starting transfers between devices: 131 us -> 92.1 us  [the longest x18 90.8 us: exchange(): return lax.ppermute(value, 'ctx', pairs)]
    all_to_all x0 -> x1, starting transfers between devices: none -> 26.8 us  [block_spans(): spans = lax.all_to_all(mine, 'ctx', split_axis=0, concat_axis=0, tiled=True)]
    all_to_all x1 -> x2, starting transfers between devices: 4.41 us -> 13.3 us  [sum_at_owner(): lax.all_to_all(pieces, axis, split_axis=0, concat_axis=0, tiled=True)]
    dot_general x30, matrix products: 17.9 us -> 23.2 us  [the longest x7 8.59 us: mixer(): jnp.einsum('thp,hpn->tn', weighted[bit].astype(jnp.float32), buckets[bit]...]
  transfers between devices with their start and end apart: 22 -> 22, of which waited for: 19 -> 10; matrix products, arithmetic and copies ran while one was open for 6% -> 14% of each run, Pallas kernels for 0% -> 0%
where the time goes in v1:
time: 218 us; the launch traced here: 216 us
  starting transfers between devices  132 us (61%)
  waiting for transfers between devices  47.2 us (22%)
  matrix products  23.2 us (11%)
  other arithmetic  7.44 us (3%)
  local copies, waits for them, and re-layouts  4.46 us (2%)
    ppermute x18, starting transfers between devices, exchange(): return lax.ppermute(value, 'ctx', pairs)  90.8 us
    ppermute x18, waiting for transfers between devices, exchange(): return lax.ppermute(value, 'ctx', pairs)  39.7 us
    all_to_all x1, starting transfers between devices, block_spans(): spans = lax.all_to_all(mine, 'ctx', split_axis=0, concat_axis=0, tiled=True)  26.8 us
    all_to_all x2, starting transfers between devices, sum_at_owner(): lax.all_to_all(pieces, axis, split_axis=0, concat_axis=0, tiled=True)  13.3 us
    dot_general x7, matrix products, mixer(): jnp.einsum('thp,hpn->tn', weighted[bit].astype(jnp.float32), buckets[bit]...  8.59 us
    all_to_all x2, waiting for transfers between devices, sum_at_owner(): lax.all_to_all(pieces, axis, split_axis=0, concat_axis=0, tiled=True)  6.1 us
  transfers between devices with their start and end apart: 22, of which 10 were waited for; matrix products, arithmetic and copies ran while one was open for 14% of the time, Pallas kernels for 0%

profile of v1, /device:TPU:1, one launch (start us, length us, event | category | flops | bytes accessed | tf_op | source)
XLA Modules:
  0.0 216.2 jit_solution(4445507015860663186)
XLA Ops:
  3.2 26.8 %all-to-all-start = ((f32[128,1,10]{2,1,0:T(1,128)}), f32[128,1,10]{2,1,0:T(1,128)S(1)}, u32[]{:S(2)}, u32[]{:S(2)}) async-start(f32[128,1,10]{2,1,0:T(1,128)} %broadcast_in_dim.203), calls=%async_computation | async-start | bytes 131072 | tf_op jit(solution)/shard_map/all_to_all | solution.py:25
  30.0 0.9 fusion.76
  31.8 2.5 %collective-permute-start = (f32[10,64,128]{2,1,0:T(8,128)S(1)}, f32[10,64,128]{2,1,0:T(8,128)S(1)}, u32[]{:S(2)}, u32[]{:S(2)}) collective-permute-start(f32[10,64,128]{2,1,0:T(8,128)S(1)} %convolution_bitcast_fusion.9), channel_id=1, source_target_pairs={{0,8},{8,0},{16,24},{24,16},{32,40},{40,32},{48,56},{56,48},{64,72... | collective-permute-start | bytes 983048 | tf_op jit(solution)/shard_map/ppermute | solution.py:9
  34.5 1.0 fusion.47
  35.5 1.3 collective-permute-start.18
  37.0 1.3 convert_reduce_fusion
  39.5 1.9 fusion.25
  41.4 1.9 convolution_bitcast_fusion.1
  43.5 1.5 all-to-all-done
  46.0 5.9 %collective-permute-start.9 = (f32[10,64,128]{2,1,0:T(8,128)S(1)}, f32[10,64,128]{2,1,0:T(8,128)S(1)}, u32[]{:S(2)}, u32[]{:S(2)}) collective-permute-start(f32[10,64,128]{2,1,0:T(8,128)S(1)} %convolution_add_fusion.1), channel_id=1, source_target_pairs={{0,512},{8,520},{16,528},{24,536},{32,544},{40,552},{48,560},{56,5... | collective-permute-start | bytes 983048 | tf_op jit(solution)/shard_map/ppermute | solution.py:9
  52.9 4.0 %collective-permute-start.1 = (f32[5,64,128]{2,1,0:T(8,128)S(1)}, f32[5,64,128]{2,1,0:T(8,128)S(1)}, u32[]{:S(2)}, u32[]{:S(2)}) collective-permute-start(f32[5,64,128]{2,1,0:T(8,128)S(1)} %constant_dynamic-slice_fusion), channel_id=1, source_target_pairs={{0,16},{8,24},{16,0},{24,8},{32,48},{40,56},{48,32},{56,40},{64,80... | collective-permute-start | bytes 491528 | tf_op jit(solution)/shard_map/ppermute | solution.py:9
  57.1 4.6 %collective-permute-start.13 = (f32[3,10,32,128]{3,2,1,0:T(8,128)S(1)}, f32[3,10,32,128]{3,2,1,0:T(8,128)S(1)}, u32[]{:S(2)}, u32[]{:S(2)}) collective-permute-start(f32[3,10,32,128]{3,2,1,0:T(8,128)S(1)} %pad_maximum_fusion), channel_id=1, source_target_pairs={{0,8},{8,0},{16,24},{24,16},{32,40},{40,32},{48,56},{56,48},{64,72... | collective-permute-start | bytes 1474568 | tf_op jit(solution)/shard_map/ppermute | solution.py:9
  61.9 7.0 %collective-permute-start.2 = (f32[5,64,128]{2,1,0:T(8,128)S(1)}, f32[5,64,128]{2,1,0:T(8,128)S(1)}, u32[]{:S(2)}, u32[]{:S(2)}) collective-permute-start(f32[5,64,128]{2,1,0:T(8,128)S(1)} %multiply_add_fusion.12), channel_id=1, source_target_pairs={{0,32},{8,40},{16,48},{24,56},{32,0},{40,8},{48,16},{56,24},{64,96... | collective-permute-start | bytes 491528 | tf_op jit(solution)/shard_map/ppermute | solution.py:9
  69.2 2.4 %collective-permute-start.10 = (f32[10,64,128]{2,1,0:T(8,128)S(1)}, f32[10,64,128]{2,1,0:T(8,128)S(1)}, u32[]{:S(2)}, u32[]{:S(2)}) collective-permute-start(f32[10,64,128]{2,1,0:T(8,128)S(1)} %multiply_add_fusion.2), channel_id=1, source_target_pairs={{0,256},{8,264},{16,272},{24,280},{32,288},{40,296},{48,304},{56,3... | collective-permute-start | bytes 983048 | tf_op jit(solution)/shard_map/ppermute | solution.py:9
  71.6 4.1 %collective-permute-done.2 = f32[5,64,128]{2,1,0:T(8,128)S(1)} collective-permute-done((f32[5,64,128]{2,1,0:T(8,128)S(1)}, f32[5,64,128]{2,1,0:T(8,128)S(1)}, u32[]{:S(2)}, u32[]{:S(2)}) %collective-permute-start.2) | collective-permute-done | bytes 163872 | tf_op jit(solution)/shard_map/ppermute | solution.py:9
  75.8 15.2 %collective-permute-start.3 = (f32[2,5,64,128]{3,2,1,0:T(8,128)S(1)}, f32[2,5,64,128]{3,2,1,0:T(8,128)S(1)}, u32[]{:S(2)}, u32[]{:S(2)}) collective-permute-start(f32[2,5,64,128]{3,2,1,0:T(8,128)S(1)} %pad_maximum_fusion.1), channel_id=1, source_target_pairs={{0,8},{8,0},{16,24},{24,16},{32,40},{40,32},{48,56},{56,48},{64,72... | collective-permute-start | bytes 983048 | tf_op jit(solution)/shard_map/ppermute | solution.py:9
  91.0 4.3 %collective-permute-start.4 = (f32[5,64,128]{2,1,0:T(8,128)S(1)}, f32[5,64,128]{2,1,0:T(8,128)S(1)}, u32[]{:S(2)}, u32[]{:S(2)}) collective-permute-start(f32[5,64,128]{2,1,0:T(8,128)S(1)} %multiply_add_fusion.11), channel_id=1, source_target_pairs={{0,64},{8,72},{16,80},{24,88},{32,96},{40,104},{48,112},{56,120},{... | collective-permute-start | bytes 491528 | tf_op jit(solution)/shard_map/ppermute | solution.py:9
  95.6 2.3 %collective-permute-start.11 = (f32[10,64,128]{2,1,0:T(8,128)S(1)}, f32[10,64,128]{2,1,0:T(8,128)S(1)}, u32[]{:S(2)}, u32[]{:S(2)}) collective-permute-start(f32[10,64,128]{2,1,0:T(8,128)S(1)} %multiply_add_fusion), channel_id=1, source_target_pairs={{0,128},{8,136},{16,144},{24,152},{32,160},{40,168},{48,176},{56,1... | collective-permute-start | bytes 983048 | tf_op jit(solution)/shard_map/ppermute | solution.py:9
  97.9 12.0 %collective-permute-done.4 = f32[5,64,128]{2,1,0:T(8,128)S(1)} collective-permute-done((f32[5,64,128]{2,1,0:T(8,128)S(1)}, f32[5,64,128]{2,1,0:T(8,128)S(1)}, u32[]{:S(2)}, u32[]{:S(2)}) %collective-permute-start.4) | collective-permute-done | bytes 163872 | tf_op jit(solution)/shard_map/ppermute | solution.py:9
  109.9 5.6 %collective-permute-start.5 = (f32[5,64,128]{2,1,0:T(8,128)S(1)}, f32[5,64,128]{2,1,0:T(8,128)S(1)}, u32[]{:S(2)}, u32[]{:S(2)}) collective-permute-start(f32[5,64,128]{2,1,0:T(8,128)S(1)} %collective-permute-done.4), channel_id=1, source_target_pairs={{0,8},{8,0},{16,24},{24,16},{32,40},{40,32},{48,56},{56,48},{64,72... | collective-permute-start | bytes 491528 | tf_op jit(solution)/shard_map/ppermute | solution.py:9
  115.6 5.7 %collective-permute-done.5 = f32[5,64,128]{2,1,0:T(8,128)S(1)} collective-permute-done((f32[5,64,128]{2,1,0:T(8,128)S(1)}, f32[5,64,128]{2,1,0:T(8,128)S(1)}, u32[]{:S(2)}, u32[]{:S(2)}) %collective-permute-start.5) | collective-permute-done | bytes 163872 | tf_op jit(solution)/shard_map/ppermute | solution.py:9
  121.5 2.3 %collective-permute-start.6 = (f32[10,64,128]{2,1,0:T(8,128)S(1)}, f32[10,64,128]{2,1,0:T(8,128)S(1)}, u32[]{:S(2)}, u32[]{:S(2)}) collective-permute-start(f32[10,64,128]{2,1,0:T(8,128)S(1)} %get-tuple-element.112), channel_id=1, source_target_pairs={{0,128},{8,136},{16,144},{24,152},{32,160},{40,168},{48,176},{56,1... | collective-permute-start | bytes 983048 | tf_op jit(solution)/shard_map/ppermute | solution.py:9
  125.3 1.9 collective-permute-start.12
  127.7 1.2 convolution_bitcast_fusion.13
  128.9 3.3 %collective-permute-done.12 = f32[10,32,128]{2,1,0:T(8,128)S(1)} collective-permute-done((f32[10,32,128]{2,1,0:T(8,128)S(1)}, f32[10,32,128]{2,1,0:T(8,128)S(1)}, u32[]{:S(2)}, u32[]{:S(2)}) %collective-permute-start.12) | collective-permute-done | bytes 163872 | tf_op jit(solution)/shard_map/ppermute | solution.py:9
  132.3 6.5 %collective-permute-start.14 = (f32[10,32,128]{2,1,0:T(8,128)S(1)}, f32[10,32,128]{2,1,0:T(8,128)S(1)}, u32[]{:S(2)}, u32[]{:S(2)}) collective-permute-start(f32[10,32,128]{2,1,0:T(8,128)S(1)} %get-tuple-element.104), channel_id=1, source_target_pairs={{0,64},{8,72},{16,80},{24,88},{32,96},{40,104},{48,112},{56,120},{... | collective-permute-start | bytes 491528 | tf_op jit(solution)/shard_map/ppermute | solution.py:9
  138.8 1.2 convolution_bitcast_fusion.14
  140.0 1.2 convolution_bitcast_fusion.15
  141.1 6.1 %collective-permute-done.14 = f32[10,32,128]{2,1,0:T(8,128)S(1)} collective-permute-done((f32[10,32,128]{2,1,0:T(8,128)S(1)}, f32[10,32,128]{2,1,0:T(8,128)S(1)}, u32[]{:S(2)}, u32[]{:S(2)}) %collective-permute-start.14) | collective-permute-done | bytes 163872 | tf_op jit(solution)/shard_map/ppermute | solution.py:9
  147.4 1.9 collective-permute-start.15
  149.4 2.4 %collective-permute-start.7 = (f32[10,64,128]{2,1,0:T(8,128)S(1)}, f32[10,64,128]{2,1,0:T(8,128)S(1)}, u32[]{:S(2)}, u32[]{:S(2)}) collective-permute-start(f32[10,64,128]{2,1,0:T(8,128)S(1)} %multiply_add_fusion.5), channel_id=1, source_target_pairs={{0,256},{8,264},{16,272},{24,280},{32,288},{40,296},{48,304},{56,3... | collective-permute-start | bytes 983048 | tf_op jit(solution)/shard_map/ppermute | solution.py:9
  151.8 1.2 convolution_bitcast_fusion.12
  153.0 7.3 %collective-permute-done.15 = f32[10,32,128]{2,1,0:T(8,128)S(1)} collective-permute-done((f32[10,32,128]{2,1,0:T(8,128)S(1)}, f32[10,32,128]{2,1,0:T(8,128)S(1)}, u32[]{:S(2)}, u32[]{:S(2)}) %collective-permute-start.15) | collective-permute-done | bytes 163872 | tf_op jit(solution)/shard_map/ppermute | solution.py:9
  160.5 12.4 %collective-permute-start.16 = (f32[10,32,128]{2,1,0:T(8,128)S(1)}, f32[10,32,128]{2,1,0:T(8,128)S(1)}, u32[]{:S(2)}, u32[]{:S(2)}) collective-permute-start(f32[10,32,128]{2,1,0:T(8,128)S(1)} %get-tuple-element.102), channel_id=1, source_target_pairs={{0,16},{8,24},{16,0},{24,8},{32,48},{40,56},{48,32},{56,40},{64,80... | collective-permute-start | bytes 491528 | tf_op jit(solution)/shard_map/ppermute | solution.py:9
  172.9 0.8 multiply_add_fusion.4
  173.7 2.6 %collective-permute-start.8 = (f32[10,64,128]{2,1,0:T(8,128)}, f32[10,64,128]{2,1,0:T(8,128)S(1)}, u32[]{:S(2)}, u32[]{:S(2)}) collective-permute-start(f32[10,64,128]{2,1,0:T(8,128)} %multiply_add_fusion.4), channel_id=1, source_target_pairs={{0,512},{8,520},{16,528},{24,536},{32,544},{40,552},{48,560},{56,5... | collective-permute-start | bytes 983048 | tf_op jit(solution)/shard_map/ppermute | solution.py:9
  176.5 7.0 %collective-permute-start.17 = (f32[10,32,128]{2,1,0:T(8,128)S(1)}, f32[10,32,128]{2,1,0:T(8,128)S(1)}, u32[]{:S(2)}, u32[]{:S(2)}) collective-permute-start(f32[10,32,128]{2,1,0:T(8,128)S(1)} %multiply_add_fusion.8), channel_id=1, source_target_pairs={{0,8},{8,0},{16,24},{24,16},{32,40},{40,32},{48,56},{56,48},{64,72... | collective-permute-start | bytes 491528 | tf_op jit(solution)/shard_map/ppermute | solution.py:9
  183.9 1.2 convolution_bitcast_fusion.11
  185.1 1.0 collective-permute-done.17
  186.2 1.1 fusion.45
  188.4 9.1 %all-to-all-start.1 = ((f32[8,32,128]{2,1,0:T(8,128)}), f32[8,32,128]{2,1,0:T(8,128)S(1)}, u32[]{:S(2)}, u32[]{:S(2)}) async-start(f32[8,32,128]{2,1,0:T(8,128)} %bitcast.43), calls=%async_computation.1 | async-start | bytes 262144 | tf_op jit(solution)/shard_map/all_to_all | solution.py:19
  197.5 1.7 fusion.17
  199.2 0.9 copy.38
  200.1 2.6 %all-to-all-done.1 = f32[8,32,128]{2,1,0:T(8,128)S(1)} async-done(((f32[8,32,128]{2,1,0:T(8,128)}), f32[8,32,128]{2,1,0:T(8,128)S(1)}, u32[]{:S(2)}, u32[]{:S(2)}) %all-to-all-start.1) | async-done | bytes 131104 | tf_op jit(solution)/shard_map/all_to_all | solution.py:19
  203.9 2.2 fusion.24
  206.1 4.3 %all-to-all-start.2 = ((f32[8,32,128]{2,1,0:T(8,128)}), f32[8,32,128]{2,1,0:T(8,128)S(1)}, u32[]{:S(2)}, u32[]{:S(2)}) async-start(f32[8,32,128]{2,1,0:T(8,128)} %bitcast.51), calls=%async_computation.2 | async-start | bytes 262144 | tf_op jit(solution)/shard_map/all_to_all | solution.py:19
  211.2 0.9 copy.37
  212.1 3.5 %all-to-all-done.2 = f32[8,32,128]{2,1,0:T(8,128)S(1)} async-done(((f32[8,32,128]{2,1,0:T(8,128)}), f32[8,32,128]{2,1,0:T(8,128)S(1)}, u32[]{:S(2)}, u32[]{:S(2)}) %all-to-all-start.2) | async-done | bytes 131104 | tf_op jit(solution)/shard_map/all_to_all | solution.py:19
  (117 shorter events, 14.6 us)
Async XLA Ops:
  0.6 33.9 %copy-start = (bf16[256,128]{1,0:T(8,128)(2,1)S(1)}, bf16[256,128]{1,0:T(8,128)(2,1)}, u32[]{:S(2)}) copy-start(bf16[256,128]{1,0:T(8,128)(2,1)} %param.8) | copy-start | bytes 196612
  0.6 30.3 %copy-start.7 = (bf16[256,640]{1,0:T(8,128)(2,1)S(1)}, bf16[256,640]{1,0:T(8,128)(2,1)}, u32[]{:S(2)}) copy-start(bf16[256,640]{1,0:T(8,128)(2,1)} %param.6) | copy-start | bytes 983044
  1.4 29.7 %copy-start.2 = (bf16[256,128]{1,0:T(8,128)(2,1)S(1)}, bf16[256,128]{1,0:T(8,128)(2,1)}, u32[]{:S(2)}) copy-start(bf16[256,128]{1,0:T(8,128)(2,1)} %param.7) | copy-start | bytes 196612
  3.2 41.8 %all-to-all-start = ((f32[128,1,10]{2,1,0:T(1,128)}), f32[128,1,10]{2,1,0:T(1,128)S(1)}, u32[]{:S(2)}, u32[]{:S(2)}) async-start(f32[128,1,10]{2,1,0:T(1,128)} %broadcast_in_dim.203), calls=%async_computation | async-start | bytes 131072 | tf_op jit(solution)/shard_map/all_to_all | solution.py:25
  31.1 10.3 %copy-start.9 = (bf16[256,640]{0,1:T(8,128)(2,1)}, bf16[256,640]{0,1:T(8,128)(2,1)S(1)}, u32[]{:S(2)}) copy-start(bf16[256,640]{0,1:T(8,128)(2,1)S(1)} %copy.34) | copy-start | bytes 983044
  31.2 3.2 %copy-start.8 = (bf16[256,640]{1,0:T(8,128)(2,1)S(1)}, bf16[256,640]{1,0:T(8,128)(2,1)}, u32[]{:S(2)}) copy-start(bf16[256,640]{1,0:T(8,128)(2,1)} %param.11) | copy-start | bytes 983044
  31.8 20.9 %collective-permute-start = (f32[10,64,128]{2,1,0:T(8,128)S(1)}, f32[10,64,128]{2,1,0:T(8,128)S(1)}, u32[]{:S(2)}, u32[]{:S(2)}) collective-permute-start(f32[10,64,128]{2,1,0:T(8,128)S(1)} %convolution_bitcast_fusion.9), channel_id=1, source_target_pairs={{0,8},{8,0},{16,24},{24,16},{32,40},{40,32},{48,56},{56,48},{64,72... | collective-permute-start | bytes 983048 | tf_op jit(solution)/shard_map/ppermute | solution.py:9
  35.5 149.6 %collective-permute-start.18 = (f32[10,64,128]{2,1,0:T(8,128)}, f32[10,64,128]{2,1,0:T(8,128)}, u32[]{:S(2)}, u32[]{:S(2)}) collective-permute-start(f32[10,64,128]{2,1,0:T(8,128)} %fusion.47), channel_id=1, source_target_pairs={{8,0},{24,16},{40,32},{56,48},{72,64},{88,80},{104,96},{120,112},{... | collective-permute-start | bytes 983048 | tf_op jit(solution)/shard_map/ppermute | solution.py:14
  46.0 22.9 %collective-permute-start.9 = (f32[10,64,128]{2,1,0:T(8,128)S(1)}, f32[10,64,128]{2,1,0:T(8,128)S(1)}, u32[]{:S(2)}, u32[]{:S(2)}) collective-permute-start(f32[10,64,128]{2,1,0:T(8,128)S(1)} %convolution_add_fusion.1), channel_id=1, source_target_pairs={{0,512},{8,520},{16,528},{24,536},{32,544},{40,552},{48,560},{56,5... | collective-permute-start | bytes 983048 | tf_op jit(solution)/shard_map/ppermute | solution.py:9
  52.9 8.9 %collective-permute-start.1 = (f32[5,64,128]{2,1,0:T(8,128)S(1)}, f32[5,64,128]{2,1,0:T(8,128)S(1)}, u32[]{:S(2)}, u32[]{:S(2)}) collective-permute-start(f32[5,64,128]{2,1,0:T(8,128)S(1)} %constant_dynamic-slice_fusion), channel_id=1, source_target_pairs={{0,16},{8,24},{16,0},{24,8},{32,48},{40,56},{48,32},{56,40},{64,80... | collective-permute-start | bytes 491528 | tf_op jit(solution)/shard_map/ppermute | solution.py:9
  57.1 71.8 %collective-permute-start.13 = (f32[3,10,32,128]{3,2,1,0:T(8,128)S(1)}, f32[3,10,32,128]{3,2,1,0:T(8,128)S(1)}, u32[]{:S(2)}, u32[]{:S(2)}) collective-permute-start(f32[3,10,32,128]{3,2,1,0:T(8,128)S(1)} %pad_maximum_fusion), channel_id=1, source_target_pairs={{0,8},{8,0},{16,24},{24,16},{32,40},{40,32},{48,56},{56,48},{64,72... | collective-permute-start | bytes 1474568 | tf_op jit(solution)/shard_map/ppermute | solution.py:9
  61.9 13.9 %collective-permute-start.2 = (f32[5,64,128]{2,1,0:T(8,128)S(1)}, f32[5,64,128]{2,1,0:T(8,128)S(1)}, u32[]{:S(2)}, u32[]{:S(2)}) collective-permute-start(f32[5,64,128]{2,1,0:T(8,128)S(1)} %multiply_add_fusion.12), channel_id=1, source_target_pairs={{0,32},{8,40},{16,48},{24,56},{32,0},{40,8},{48,16},{56,24},{64,96... | collective-permute-start | bytes 491528 | tf_op jit(solution)/shard_map/ppermute | solution.py:9
  69.2 26.2 %collective-permute-start.10 = (f32[10,64,128]{2,1,0:T(8,128)S(1)}, f32[10,64,128]{2,1,0:T(8,128)S(1)}, u32[]{:S(2)}, u32[]{:S(2)}) collective-permute-start(f32[10,64,128]{2,1,0:T(8,128)S(1)} %multiply_add_fusion.2), channel_id=1, source_target_pairs={{0,256},{8,264},{16,272},{24,280},{32,288},{40,296},{48,304},{56,3... | collective-permute-start | bytes 983048 | tf_op jit(solution)/shard_map/ppermute | solution.py:9
  75.8 39.8 %collective-permute-start.3 = (f32[2,5,64,128]{3,2,1,0:T(8,128)S(1)}, f32[2,5,64,128]{3,2,1,0:T(8,128)S(1)}, u32[]{:S(2)}, u32[]{:S(2)}) collective-permute-start(f32[2,5,64,128]{3,2,1,0:T(8,128)S(1)} %pad_maximum_fusion.1), channel_id=1, source_target_pairs={{0,8},{8,0},{16,24},{24,16},{32,40},{40,32},{48,56},{56,48},{64,72... | collective-permute-start | bytes 983048 | tf_op jit(solution)/shard_map/ppermute | solution.py:9
  91.0 18.9 %collective-permute-start.4 = (f32[5,64,128]{2,1,0:T(8,128)S(1)}, f32[5,64,128]{2,1,0:T(8,128)S(1)}, u32[]{:S(2)}, u32[]{:S(2)}) collective-permute-start(f32[5,64,128]{2,1,0:T(8,128)S(1)} %multiply_add_fusion.11), channel_id=1, source_target_pairs={{0,64},{8,72},{16,80},{24,88},{32,96},{40,104},{48,112},{56,120},{... | collective-permute-start | bytes 491528 | tf_op jit(solution)/shard_map/ppermute | solution.py:9
  95.6 29.5 %collective-permute-start.11 = (f32[10,64,128]{2,1,0:T(8,128)S(1)}, f32[10,64,128]{2,1,0:T(8,128)S(1)}, u32[]{:S(2)}, u32[]{:S(2)}) collective-permute-start(f32[10,64,128]{2,1,0:T(8,128)S(1)} %multiply_add_fusion), channel_id=1, source_target_pairs={{0,128},{8,136},{16,144},{24,152},{32,160},{40,168},{48,176},{56,1... | collective-permute-start | bytes 983048 | tf_op jit(solution)/shard_map/ppermute | solution.py:9
  109.9 11.3 %collective-permute-start.5 = (f32[5,64,128]{2,1,0:T(8,128)S(1)}, f32[5,64,128]{2,1,0:T(8,128)S(1)}, u32[]{:S(2)}, u32[]{:S(2)}) collective-permute-start(f32[5,64,128]{2,1,0:T(8,128)S(1)} %collective-permute-done.4), channel_id=1, source_target_pairs={{0,8},{8,0},{16,24},{24,16},{32,40},{40,32},{48,56},{56,48},{64,72... | collective-permute-start | bytes 491528 | tf_op jit(solution)/shard_map/ppermute | solution.py:9
  121.5 27.8 %collective-permute-start.6 = (f32[10,64,128]{2,1,0:T(8,128)S(1)}, f32[10,64,128]{2,1,0:T(8,128)S(1)}, u32[]{:S(2)}, u32[]{:S(2)}) collective-permute-start(f32[10,64,128]{2,1,0:T(8,128)S(1)} %get-tuple-element.112), channel_id=1, source_target_pairs={{0,128},{8,136},{16,144},{24,152},{32,160},{40,168},{48,176},{56,1... | collective-permute-start | bytes 983048 | tf_op jit(solution)/shard_map/ppermute | solution.py:9
  125.3 6.9 %collective-permute-start.12 = (f32[10,32,128]{2,1,0:T(8,128)S(1)}, f32[10,32,128]{2,1,0:T(8,128)S(1)}, u32[]{:S(2)}, u32[]{:S(2)}) collective-permute-start(f32[10,32,128]{2,1,0:T(8,128)S(1)} %slice_select_fusion), channel_id=1, source_target_pairs={{0,8},{8,0},{16,24},{24,16},{32,40},{40,32},{48,56},{56,48},{64,72... | collective-permute-start | bytes 491528 | tf_op jit(solution)/shard_map/ppermute | solution.py:9
  132.3 15.0 %collective-permute-start.14 = (f32[10,32,128]{2,1,0:T(8,128)S(1)}, f32[10,32,128]{2,1,0:T(8,128)S(1)}, u32[]{:S(2)}, u32[]{:S(2)}) collective-permute-start(f32[10,32,128]{2,1,0:T(8,128)S(1)} %get-tuple-element.104), channel_id=1, source_target_pairs={{0,64},{8,72},{16,80},{24,88},{32,96},{40,104},{48,112},{56,120},{... | collective-permute-start | bytes 491528 | tf_op jit(solution)/shard_map/ppermute | solution.py:9
  147.4 13.0 %collective-permute-start.15 = (f32[10,32,128]{2,1,0:T(8,128)S(1)}, f32[10,32,128]{2,1,0:T(8,128)S(1)}, u32[]{:S(2)}, u32[]{:S(2)}) collective-permute-start(f32[10,32,128]{2,1,0:T(8,128)S(1)} %fusion.73), channel_id=1, source_target_pairs={{0,32},{8,40},{16,48},{24,56},{32,0},{40,8},{48,16},{56,24},{64,96... | collective-permute-start | bytes 491528 | tf_op jit(solution)/shard_map/ppermute | solution.py:9
  149.4 23.5 %collective-permute-start.7 = (f32[10,64,128]{2,1,0:T(8,128)S(1)}, f32[10,64,128]{2,1,0:T(8,128)S(1)}, u32[]{:S(2)}, u32[]{:S(2)}) collective-permute-start(f32[10,64,128]{2,1,0:T(8,128)S(1)} %multiply_add_fusion.5), channel_id=1, source_target_pairs={{0,256},{8,264},{16,272},{24,280},{32,288},{40,296},{48,304},{56,3... | collective-permute-start | bytes 983048 | tf_op jit(solution)/shard_map/ppermute | solution.py:9
  160.5 15.9 %collective-permute-start.16 = (f32[10,32,128]{2,1,0:T(8,128)S(1)}, f32[10,32,128]{2,1,0:T(8,128)S(1)}, u32[]{:S(2)}, u32[]{:S(2)}) collective-permute-start(f32[10,32,128]{2,1,0:T(8,128)S(1)} %get-tuple-element.102), channel_id=1, source_target_pairs={{0,16},{8,24},{16,0},{24,8},{32,48},{40,56},{48,32},{56,40},{64,80... | collective-permute-start | bytes 491528 | tf_op jit(solution)/shard_map/ppermute | solution.py:9
  173.7 29.6 %collective-permute-start.8 = (f32[10,64,128]{2,1,0:T(8,128)}, f32[10,64,128]{2,1,0:T(8,128)S(1)}, u32[]{:S(2)}, u32[]{:S(2)}) collective-permute-start(f32[10,64,128]{2,1,0:T(8,128)} %multiply_add_fusion.4), channel_id=1, source_target_pairs={{0,512},{8,520},{16,528},{24,536},{32,544},{40,552},{48,560},{56,5... | collective-permute-start | bytes 983048 | tf_op jit(solution)/shard_map/ppermute | solution.py:9
  176.5 9.7 %collective-permute-start.17 = (f32[10,32,128]{2,1,0:T(8,128)S(1)}, f32[10,32,128]{2,1,0:T(8,128)S(1)}, u32[]{:S(2)}, u32[]{:S(2)}) collective-permute-start(f32[10,32,128]{2,1,0:T(8,128)S(1)} %multiply_add_fusion.8), channel_id=1, source_target_pairs={{0,8},{8,0},{16,24},{24,16},{32,40},{40,32},{48,56},{56,48},{64,72... | collective-permute-start | bytes 491528 | tf_op jit(solution)/shard_map/ppermute | solution.py:9
  183.9 3.3 %copy-start.10 = (bf16[256,640]{0,1:T(8,128)(2,1)S(1)}, bf16[256,640]{0,1:T(8,128)(2,1)}, u32[]{:S(2)}) copy-start(bf16[256,640]{0,1:T(8,128)(2,1)} %copy-done.9) | copy-start | bytes 983044
  188.4 14.3 %all-to-all-start.1 = ((f32[8,32,128]{2,1,0:T(8,128)}), f32[8,32,128]{2,1,0:T(8,128)S(1)}, u32[]{:S(2)}, u32[]{:S(2)}) async-start(f32[8,32,128]{2,1,0:T(8,128)} %bitcast.43), calls=%async_computation.1 | async-start | bytes 262144 | tf_op jit(solution)/shard_map/all_to_all | solution.py:19
  199.1 4.7 %copy-start.3 = (f32[256,128]{1,0:T(8,128)S(1)}, f32[256,128]{1,0:T(8,128)}, u32[]{:S(2)}) copy-start(f32[256,128]{1,0:T(8,128)} %convolution_bitcast_fusion.13) | copy-start | bytes 393220
  199.1 4.7 %copy-start.4 = (f32[256,128]{1,0:T(8,128)S(1)}, f32[256,128]{1,0:T(8,128)}, u32[]{:S(2)}) copy-start(f32[256,128]{1,0:T(8,128)} %convolution_bitcast_fusion.14) | copy-start | bytes 393220
  200.1 3.8 %copy-start.5 = (f32[256,128]{1,0:T(8,128)S(1)}, f32[256,128]{1,0:T(8,128)}, u32[]{:S(2)}) copy-start(f32[256,128]{1,0:T(8,128)} %convolution_bitcast_fusion.15) | copy-start | bytes 393220
  200.1 3.8 %copy-start.6 = (f32[256,128]{1,0:T(8,128)S(1)}, f32[256,128]{1,0:T(8,128)}, u32[]{:S(2)}) copy-start(f32[256,128]{1,0:T(8,128)} %convolution_bitcast_fusion.12) | copy-start | bytes 393220
  206.1 4.7 %copy-start.1 = (f32[256,10,64]{0,2,1:T(8,128)S(1)}, f32[256,10,64]{0,2,1:T(8,128)}, u32[]{:S(2)}) copy-start(f32[256,10,64]{0,2,1:T(8,128)} %convolution_bitcast_fusion.1) | copy-start | bytes 1966084
  206.1 9.5 %all-to-all-start.2 = ((f32[8,32,128]{2,1,0:T(8,128)}), f32[8,32,128]{2,1,0:T(8,128)S(1)}, u32[]{:S(2)}, u32[]{:S(2)}) async-start(f32[8,32,128]{2,1,0:T(8,128)} %bitcast.51), calls=%async_computation.2 | async-start | bytes 262144 | tf_op jit(solution)/shard_map/all_to_all | solution.py:19

commit v2 on v1

--- a/solution.py
+++ b/solution.py
@@ -16,39 +16,46 @@
 
 def sum_at_owner(value, axis):
     pieces = value.reshape(lax.axis_size(axis), -1, value.shape[1])
-    return lax.all_to_all(pieces, axis, split_axis=0, concat_axis=0, tiled=True).sum(axis=0)
-
-
-def block_spans(total, shard_index, level_count):
-    size = 2**level_count
-    mine = jnp.broadcast_to(total[None, None, :], (size, 1, total.shape[0]))
-    spans = lax.all_to_all(mine, "ctx", split_axis=0, concat_axis=0, tiled=True)
-    spans = spans[:, 0]
-    stretch = jnp.arange(size)[:, None]
-    own_spans, peer_spans, offsets = ([], [], [])
-    offset = jnp.zeros_like(total)
-    for bit in range(level_count):
-        block = shard_index // 2**bit
-        own = jnp.sum(jnp.where(stretch // 2**bit == block, spans, 0.0), axis=0)
-        peer = jnp.sum(jnp.where(stretch // 2**bit == (block ^ 1), spans, 0.0), axis=0)
-        own_spans.append(own)
-        peer_spans.append(peer)
-        offsets.append(offset)
+    arrived = lax.all_to_all(pieces, axis, split_axis=0, concat_axis=0, tiled=True)
+    return arrived.sum(axis=0)
+
+
+def all_totals(total, groups):
+    mine = jnp.broadcast_to(total[None, None, :], (len(groups[0]), 1, total.shape[0]))
+    got = lax.all_to_all(mine, "ctx", 0, 0, axis_index_groups=groups, tiled=True)
+    return got[:, 0]
+
+
+def sum_where(mask, spans):
+    return jnp.sum(jnp.where(mask[:, None], spans, 0.0), axis=0)
+
+
+def sibling_spans(spans, position):
+    member = jnp.arange(spans.shape[0])
+    levels = []
+    offset = jnp.zeros_like(spans[0])
+    for bit in range(spans.shape[0].bit_length() - 1):
+        block = position // 2**bit
+        own = sum_where(member // 2**bit == block, spans)
+        peer = sum_where(member // 2**bit == (block ^ 1), spans)
+        levels.append((own, peer, offset))
         offset = offset + jnp.where(block % 2 == 1, peer, 0.0)
-    return own_spans, peer_spans, offsets
+    return levels, offset
 
 
 Z_BITS = 4
 
+GATHERS = ((1, 2, 3), (4, 5), (6,))
+
 
 class Side:
-    def __init__(self, keep, pull, shard_index):
-        keep, pull, shard_index = lax.optimization_barrier((keep, pull, shard_index))
-        self.given = (keep, pull, shard_index)
+    def __init__(self, *stages):
+        self.given = tuple(lax.optimization_barrier(stage) for stage in stages)
+        self.place = self.given[0][2]
         self.keep, self.pull = (
-            [factor[:, None, None] for factor in factors] for factors in (keep, pull)
+            [factor[:, None, None] for stage in self.given for factor in stage[part]]
+            for part in (0, 1)
         )
-        self.place = shard_index % 2
 
     def join(self, bit, block, peer):
         return self.keep[bit] * block + self.pull[bit] * peer
@@ -71,14 +78,18 @@
         return lax.dynamic_slice_in_dim(ring, self.place * half, 2 * half, axis=0)
 
 
+def other_half(value, place):
+    half = value.shape[1] // 2
+    return jnp.where(place == 1, value[:, :half], value[:, half:])
+
+
 class Down(Side):
     def mine(self, value):
         half = value.shape[1] // 2
         return jnp.where(self.place == 1, value[:, half:], value[:, :half])
 
     def theirs(self, value):
-        half = value.shape[1] // 2
-        return jnp.where(self.place == 1, value[:, :half], value[:, half:])
+        return other_half(value, self.place)
 
     def whole(self, own_half, other_half):
         ahead = jnp.concatenate([own_half, other_half], axis=1)
@@ -97,60 +108,106 @@
     total = running[:, -1]
     shard_index = lax.axis_index("ctx")
     level_count = lax.axis_size("ctx").bit_length() - 1
-    own_spans, peer_spans, offsets = block_spans(total, shard_index, level_count)
+    ring = 2**Z_BITS
+    rows = 2 ** (level_count - Z_BITS)
+    along_z = [[row * ring + place for place in range(ring)] for row in range(rows)]
+    along_y = [[row * ring + place for row in range(rows)] for place in range(ring)]
+    z_place, y_place = (shard_index % ring, shard_index // ring)
+    z_spans = all_totals(total, along_z)
     is_right = [shard_index // 2**bit % 2 == 1 for bit in range(level_count)]
-    keep = [
-        jnp.where(is_right[bit], 1.0, jnp.exp(peer_spans[bit])) for bit in range(level_count)
-    ]
-    pull = [jnp.where(is_right[bit], jnp.exp(own_spans[bit]), 1.0) for bit in range(level_count)]
-    up = Up(keep, pull, shard_index)
+
+    def factors(levels, first_bit):
+        right = is_right[first_bit : first_bit + len(levels)]
+        keep = [jnp.where(r, 1.0, jnp.exp(peer)) for r, (_, peer, _) in zip(right, levels)]
+        pull = [jnp.where(r, jnp.exp(own), 1.0) for r, (own, _, _) in zip(right, levels)]
+        return keep, pull
+
+    z_levels, z_prefix = sibling_spans(z_spans, z_place)
+    member = jnp.arange(ring)
+    own_reach = jnp.exp(sum_where(member < z_place, z_spans))
+    peer_reach = jnp.exp(sum_where(member < (z_place ^ 1), z_spans))
+    row_total = jnp.sum(z_spans, axis=0)
+    z_factors, z_offsets, z_prefix, reaches, row_total = lax.optimization_barrier(
+        (
+            factors(z_levels, 0),
+            [level[2] for level in z_levels],
+            z_prefix,
+            (own_reach, peer_reach),
+            row_total,
+        )
+    )
+    own_reach, peer_reach = (reach[:, None, None] for reach in reaches)
+    y_spans = all_totals(row_total, along_y)
+    y_levels, _ = sibling_spans(y_spans, y_place)
+    offsets = z_offsets + [z_prefix + level[2] for level in y_levels]
+    up = Up((*z_factors, shard_index % 2), factors(y_levels, Z_BITS))
     down = Down(*up.given)
 
     to_end = jnp.exp(total[:, None] - running)
     written = (to_end[:, :, None] * state_write.astype(jnp.float32)[None]).astype(jnp.bfloat16)
     state = jnp.einsum("uhp,hun->hpn", inputs, written, preferred_element_type=jnp.float32)
-    coefficients, weighted, level_grads = ([], [], [])
-    for bit in range(level_count):
-        coeff = jnp.where(
-            is_right[bit], scaled[bit + 1] * jnp.exp(running + offsets[bit][:, None]), 0.0
-        )
-        coefficients.append(coeff.T[:, :, None])
-        weighted.append((coefficients[bit] * cotangent.astype(jnp.float32)).astype(jnp.bfloat16))
-        level_grads.append(
-            jnp.einsum("thp,tn->hpn", weighted[bit], state_read, preferred_element_type=jnp.float32)
-        )
-    buckets = [exchange(state, 0)]
-    pair_state = up.join(0, state, buckets[0])
-    half_state = up.mine(pair_state)
-    half_buckets = []
-    for bit in range(1, Z_BITS):
-        half_buckets.append(exchange(half_state, bit))
-        half_state = up.join_half(bit, half_state, half_buckets[-1])
-    early = exchange(jnp.stack(half_buckets[:-1]), 0)
-    late = exchange(half_buckets[-1], 0)
-    block_state = pair_state
-    for bit in range(1, Z_BITS):
-        other_half = late if bit == Z_BITS - 1 else early[bit - 1]
-        buckets.append(up.whole(half_buckets[bit - 1], other_half))
-        block_state = up.join(bit, block_state, buckets[bit])
-    for bit in range(Z_BITS, level_count):
-        buckets.append(exchange(block_state, bit))
-        if bit + 1 < level_count:
-            block_state = up.join(bit, block_state, buckets[bit])
-    carried = jnp.zeros_like(state)
-
-    def step_down(bit, carried, level_grad):
-        incoming = exchange(down.pull[bit] * carried + level_grad, bit)
-        return down.keep[bit] * carried + incoming
-
+
+    def coefficient(level, log_reach, bit, place):
+        right = place // 2**bit % 2 == 1
+        return jnp.where(right, level * jnp.exp(log_reach), 0.0).T[:, :, None]
+
+    def weigh(coeff):
+        return (coeff * cotangent.astype(jnp.float32)).astype(jnp.bfloat16)
+
+    def bucket_grad(part):
+        return jnp.einsum("thp,tn->hpn", part, state_read, preferred_element_type=jnp.float32)
+
+    near, far = (range(1, Z_BITS), range(Z_BITS, level_count))
+    start = lax.optimization_barrier((running, scaled[Z_BITS + 1 :], shard_index))
+    early_grads = {
+        bit: bucket_grad(weigh(coefficient(start[1][bit - Z_BITS], start[0], bit, start[2])))
+        for bit in far
+    }
+    early_sent = jnp.stack([other_half(early_grads[bit], start[2] % 2) for bit in far])
+    coefficients, weighted = ([], [])
+    *start, state, early_sent = lax.optimization_barrier((*start, state, early_sent))
+    for bit in range(Z_BITS):
+        log_reach = start[0] + offsets[bit][:, None] if bit else start[0]
+        coefficients.append(coefficient(scaled[bit + 1], log_reach, bit, start[2]))
+        weighted.append(weigh(coefficients[bit]))
+    level_grads = [bucket_grad(part) for part in weighted]
+    *start, row_offsets, coefficients = lax.optimization_barrier(
+        (*start, offsets[Z_BITS:], coefficients)
+    )
+    for bit in far:
+        log_reach = start[0] + row_offsets[bit - Z_BITS][:, None]
+        coefficients.append(coefficient(start[1][bit - Z_BITS], log_reach, bit, start[2]))
+        weighted.append(weigh(coefficients[bit]))
+    buckets = {0: exchange(state, 0)}
+    half_state = up.mine(up.join(0, state, buckets[0]))
+    half_buckets = {}
+    for bit in range(1, level_count):
+        half_buckets[bit] = exchange(half_state, bit)
+        half_state = up.join_half(bit, half_state, half_buckets[bit])
+    for bits in GATHERS:
+        others = exchange(jnp.stack([half_buckets[bit] for bit in bits]), 0)
+        for place, bit in enumerate(bits):
+            buckets[bit] = up.whole(half_buckets[bit], others[place])
     first_grads = to_left(level_grads[0])
-    half_grads = exchange(jnp.stack([down.theirs(level_grads[bit]) for bit in range(1, Z_BITS)]), 0)
-    for bit in reversed(range(Z_BITS, level_count)):
-        carried = step_down(bit, carried, level_grads[bit])
-    half_carried = down.mine(carried) + exchange(down.theirs(carried), 0)
-    for bit in reversed(range(1, Z_BITS)):
-        half_grad = down.mine(level_grads[bit]) + half_grads[bit - 1]
-        half_carried = step_down(bit, half_carried, half_grad)
+    half_grads = {}
+    others = exchange(jnp.stack([down.theirs(level_grads[bit]) for bit in near]), 0)
+    for place, bit in enumerate(near):
+        half_grads[bit] = down.mine(level_grads[bit]) + others[place]
+    others = exchange(early_sent, 0)
+    y_member = jnp.arange(rows)
+    for place, bit in enumerate(far):
+        half_grads[bit] = own_reach * down.mine(early_grads[bit]) + peer_reach * others[place]
+    top = level_count - 1
+    sender = y_place ^ (rows // 2)
+    before = (y_member >= sender // (rows // 2) * (rows // 2)) & (y_member < sender)
+    row_reach = jnp.exp(sum_where(before, y_spans))[:, None, None]
+    half_carried = row_reach * exchange(half_grads[top], top)
+    for bit in reversed(range(1, top)):
+        grad = half_grads[bit]
+        if bit >= Z_BITS:
+            grad = jnp.exp(y_levels[bit - Z_BITS][2])[:, None, None] * grad
+        incoming = exchange(grad + down.pull[bit] * half_carried, bit)
+        half_carried = down.keep[bit] * half_carried + incoming
     pair_grad = down.whole(half_carried, exchange(half_carried, 0))
     dstate = down.keep[0] * pair_grad + first_grads
     scores = jnp.dot(state_read, state_write.T, preferred_element_type=jnp.float32)

time: 218 us -> 225 us (1.032); the launches traced: 216 us -> 220 us
  waiting for transfers between devices: 47.2 us -> 29.7 us
  other arithmetic: 7.44 us -> 23.2 us
  local copies, waits for them, and re-layouts: 4.46 us -> 14.8 us
  matrix products: 23.2 us -> 17.5 us
    ppermute x18 -> x19, waiting for transfers between devices: 39.7 us -> 25.9 us  [exchange(): return lax.ppermute(value, 'ctx', pairs)]
    all_to_all x2, starting transfers between devices: 13.3 us -> 23.9 us  [sum_at_owner(): lax.all_to_all(pieces, axis, split_axis=0, concat_axis=0, tiled=True)]
    ppermute x18 -> x19, starting transfers between devices: 90.8 us -> 81.3 us  [exchange(): return lax.ppermute(value, 'ctx', pairs)]
    add x6 -> x9, other arithmetic: 0.55 us -> 8.49 us  [the longest x5 5.86 us: mixer(): incoming = exchange(grad + down.pull[bit] * half_carried, bit)]
    dynamic_slice x5 -> x12, local copies, waits for them, and re-layouts: 0.32 us -> 6.3 us  [part(): return lax.dynamic_slice_in_dim(value, place * half, half, axis=0)]
    dot_general x7, matrix products: 8.59 us -> 4.34 us  [mixer(): jnp.einsum('thp,hpn->tn', weighted[bit].astype(jnp.float32), buckets[bit]...]
    unnamed x28 -> x134, local copies, waits for them, and re-layouts: 2.22 us -> 5.36 us
    all_to_all x2, waiting for transfers between devices: 6.1 us -> 3.75 us  [sum_at_owner(): lax.all_to_all(pieces, axis, split_axis=0, concat_axis=0, tiled=True)]
  transfers between devices with their start and end apart: 22 -> 24, of which waited for: 10 -> 7; matrix products, arithmetic and copies ran while one was open for 14% -> 21% of each run, Pallas kernels for 0% -> 0%
where the time goes in v2:
time: 225 us; the launch traced here: 220 us
  starting transfers between devices  133 us (59%)
  waiting for transfers between devices  29.7 us (13%)
  other arithmetic  23.2 us (10%)
  matrix products  17.5 us (8%)
  local copies, waits for them, and re-layouts  14.8 us (7%)
  between operations  2.49 us (1%)
    ppermute x19, starting transfers between devices, exchange(): return lax.ppermute(value, 'ctx', pairs)  81.3 us
    all_to_all x2, starting transfers between devices, all_totals(): lax.all_to_all(mine, 'ctx', 0, 0, axis_index_groups=groups, tiled=True)  26.2 us
    ppermute x19, waiting for transfers between devices, exchange(): return lax.ppermute(value, 'ctx', pairs)  25.9 us
    all_to_all x2, starting transfers between devices, sum_at_owner(): lax.all_to_all(pieces, axis, split_axis=0, concat_axis=0, tiled=True)  23.9 us
    dynamic_slice x12, local copies, waits for them, and re-layouts, part(): return lax.dynamic_slice_in_dim(value, place * half, half, axis=0)  6.3 us
    add x5, other arithmetic, mixer(): incoming = exchange(grad + down.pull[bit] * half_carried, bit)  5.86 us
    unnamed x134, local copies, waits for them, and re-layouts  5.36 us
  transfers between devices with their start and end apart: 24, of which 7 were waited for; matrix products, arithmetic and copies ran while one was open for 21% of the time, Pallas kernels for 0%

profile of v2, /device:TPU:1, one launch (start us, length us, event | category | flops | bytes accessed | tf_op | source)
XLA Modules:
  0.0 220.4 jit_solution(5433535775063585959)
XLA Ops:
  3.1 19.4 %all-to-all-start = ((f32[16,1,10]{2,1,0:T(1,128)}), f32[16,1,10]{2,1,0:T(1,128)S(1)}, u32[]{:S(2)}, u32[]{:S(2)}) async-start(f32[16,1,10]{2,1,0:T(1,128)} %broadcast_in_dim.258), calls=%async_computation | async-start | bytes 16384 | tf_op jit(solution)/shard_map/all_to_all | solution.py:25
  22.5 0.9 fusion.98
  26.3 1.3 convolution_bitcast_fusion.9
  27.6 3.3 %collective-permute-start = (f32[10,64,128]{2,1,0:T(8,128)}, f32[10,64,128]{2,1,0:T(8,128)S(1)}, u32[]{:S(2)}, u32[]{:S(2)}) collective-permute-start(f32[10,64,128]{2,1,0:T(8,128)} %convolution_bitcast_fusion.9), channel_id=1, source_target_pairs={{0,8},{8,0},{16,24},{24,16},{32,40},{40,32},{48,56},{56,48},{64,72... | collective-permute-start | bytes 983048 | tf_op jit(solution)/shard_map/ppermute | solution.py:9
  30.9 2.0 collective-permute-start.10
  34.4 1.3 convert_reduce_fusion
  37.7 1.0 fusion.25
  44.5 6.8 %all-to-all-start.1 = ((f32[8,1,10]{2,1,0:T(1,128)}), f32[8,1,10]{2,1,0:T(1,128)S(1)}, u32[]{:S(2)}, u32[]{:S(2)}) async-start(f32[8,1,10]{2,1,0:T(1,128)} %broadcast_in_dim.270), calls=%async_computation.1 | async-start | bytes 8192 | tf_op jit(solution)/shard_map/all_to_all | solution.py:25
  54.7 3.3 %collective-permute-start.14 = (f32[3,10,32,128]{3,2,1,0:T(8,128)}, f32[3,10,32,128]{3,2,1,0:T(8,128)}, u32[]{:S(2)}, u32[]{:S(2)}) collective-permute-start(f32[3,10,32,128]{3,2,1,0:T(8,128)} %pad_maximum_fusion.2), channel_id=1, source_target_pairs={{0,8},{8,0},{16,24},{24,16},{32,40},{40,32},{48,56},{56,48},{64,72... | collective-permute-start | bytes 1474568 | tf_op jit(solution)/shard_map/ppermute | solution.py:9
  58.0 1.0 fusion.71
  59.0 1.3 collective-permute-start.19
  61.6 1.7 fusion.97
  63.2 4.0 %collective-permute-start.1 = (f32[5,64,128]{2,1,0:T(8,128)}, f32[5,64,128]{2,1,0:T(8,128)S(1)}, u32[]{:S(2)}, u32[]{:S(2)}) collective-permute-start(f32[5,64,128]{2,1,0:T(8,128)} %fusion.97), channel_id=1, source_target_pairs={{0,16},{8,24},{16,0},{24,8},{32,48},{40,56},{48,32},{56,40},{64,80... | collective-permute-start | bytes 491528 | tf_op jit(solution)/shard_map/ppermute | solution.py:9
  69.8 1.4 collective-permute-done.1
  71.3 1.0 multiply_add_fusion.9
  72.3 7.0 %collective-permute-start.2 = (f32[5,64,128]{2,1,0:T(8,128)S(1)}, f32[5,64,128]{2,1,0:T(8,128)S(1)}, u32[]{:S(2)}, u32[]{:S(2)}) collective-permute-start(f32[5,64,128]{2,1,0:T(8,128)S(1)} %multiply_add_fusion.9), channel_id=1, source_target_pairs={{0,32},{8,40},{16,48},{24,56},{32,0},{40,8},{48,16},{56,24},{64,96... | collective-permute-start | bytes 491528 | tf_op jit(solution)/shard_map/ppermute | solution.py:9
  79.3 1.0 fusion.96
  80.4 7.1 %collective-permute-start.11 = (f32[10,32,128]{2,1,0:T(8,128)S(1)}, f32[10,32,128]{2,1,0:T(8,128)S(1)}, u32[]{:S(2)}, u32[]{:S(2)}) collective-permute-start(f32[10,32,128]{2,1,0:T(8,128)S(1)} %fusion.96), channel_id=1, source_target_pairs={{0,512},{8,520},{16,528},{24,536},{32,544},{40,552},{48,560},{56,5... | collective-permute-start | bytes 491528 | tf_op jit(solution)/shard_map/ppermute | solution.py:9
  88.2 5.5 %collective-permute-start.3 = (f32[5,64,128]{2,1,0:T(8,128)S(1)}, f32[5,64,128]{2,1,0:T(8,128)S(1)}, u32[]{:S(2)}, u32[]{:S(2)}) collective-permute-start(f32[5,64,128]{2,1,0:T(8,128)S(1)} %multiply_add_fusion.8), channel_id=1, source_target_pairs={{0,64},{8,72},{16,80},{24,88},{32,96},{40,104},{48,112},{56,120},{... | collective-permute-start | bytes 491528 | tf_op jit(solution)/shard_map/ppermute | solution.py:9
  93.7 1.0 fusion.94
  94.8 3.8 %collective-permute-start.12 = (f32[10,32,128]{2,1,0:T(8,128)S(1)}, f32[10,32,128]{2,1,0:T(8,128)S(1)}, u32[]{:S(2)}, u32[]{:S(2)}) collective-permute-start(f32[10,32,128]{2,1,0:T(8,128)S(1)} %fusion.94), channel_id=1, source_target_pairs={{0,256},{8,264},{16,272},{24,280},{32,288},{40,296},{48,304},{56,3... | collective-permute-start | bytes 491528 | tf_op jit(solution)/shard_map/ppermute | solution.py:9
  98.6 4.7 %collective-permute-done.3 = f32[5,64,128]{2,1,0:T(8,128)S(1)} collective-permute-done((f32[5,64,128]{2,1,0:T(8,128)S(1)}, f32[5,64,128]{2,1,0:T(8,128)S(1)}, u32[]{:S(2)}, u32[]{:S(2)}) %collective-permute-start.3) | collective-permute-done | bytes 163872 | tf_op jit(solution)/shard_map/ppermute | solution.py:9
  103.3 2.3 %collective-permute-start.5 = (f32[5,64,128]{2,1,0:T(8,128)S(1)}, f32[5,64,128]{2,1,0:T(8,128)S(1)}, u32[]{:S(2)}, u32[]{:S(2)}) collective-permute-start(f32[5,64,128]{2,1,0:T(8,128)S(1)} %multiply_add_fusion.7), channel_id=1, source_target_pairs={{0,128},{8,136},{16,144},{24,152},{32,160},{40,168},{48,176},{56,1... | collective-permute-start | bytes 491528 | tf_op jit(solution)/shard_map/ppermute | solution.py:9
  105.7 13.5 %collective-permute-start.4 = (f32[3,5,64,128]{3,2,1,0:T(8,128)S(1)}, f32[3,5,64,128]{3,2,1,0:T(8,128)S(1)}, u32[]{:S(2)}, u32[]{:S(2)}) collective-permute-start(f32[3,5,64,128]{3,2,1,0:T(8,128)S(1)} %pad_maximum_fusion.1), channel_id=1, source_target_pairs={{0,8},{8,0},{16,24},{24,16},{32,40},{40,32},{48,56},{56,48},{64,72... | collective-permute-start | bytes 1474568 | tf_op jit(solution)/shard_map/ppermute | solution.py:9
  119.2 1.0 fusion.90
  120.3 3.4 %collective-permute-start.13 = (f32[10,32,128]{2,1,0:T(8,128)S(1)}, f32[10,32,128]{2,1,0:T(8,128)S(1)}, u32[]{:S(2)}, u32[]{:S(2)}) collective-permute-start(f32[10,32,128]{2,1,0:T(8,128)S(1)} %get-tuple-element.161), channel_id=1, source_target_pairs={{0,128},{8,136},{16,144},{24,152},{32,160},{40,168},{48,176},{56,1... | collective-permute-start | bytes 491528 | tf_op jit(solution)/shard_map/ppermute | solution.py:9
  123.8 1.9 collective-permute-start.6
  126.4 1.0 fusion.87
  127.4 6.0 %collective-permute-start.15 = (f32[10,32,128]{2,1,0:T(8,128)S(1)}, f32[10,32,128]{2,1,0:T(8,128)S(1)}, u32[]{:S(2)}, u32[]{:S(2)}) collective-permute-start(f32[10,32,128]{2,1,0:T(8,128)S(1)} %fusion.87), channel_id=1, source_target_pairs={{0,64},{8,72},{16,80},{24,88},{32,96},{40,104},{48,112},{56,120},{... | collective-permute-start | bytes 491528 | tf_op jit(solution)/shard_map/ppermute | solution.py:9
  133.5 5.8 %collective-permute-start.8 = (f32[5,64,128]{2,1,0:T(8,128)S(1)}, f32[5,64,128]{2,1,0:T(8,128)S(1)}, u32[]{:S(2)}, u32[]{:S(2)}) collective-permute-start(f32[5,64,128]{2,1,0:T(8,128)S(1)} %multiply_add_fusion.5), channel_id=1, source_target_pairs={{0,512},{8,520},{16,528},{24,536},{32,544},{40,552},{48,560},{56,5... | collective-permute-start | bytes 491528 | tf_op jit(solution)/shard_map/ppermute | solution.py:9
  139.3 4.4 %collective-permute-done.15 = f32[10,32,128]{2,1,0:T(8,128)S(1)} collective-permute-done((f32[10,32,128]{2,1,0:T(8,128)S(1)}, f32[10,32,128]{2,1,0:T(8,128)S(1)}, u32[]{:S(2)}, u32[]{:S(2)}) %collective-permute-start.15) | collective-permute-done | bytes 163872 | tf_op jit(solution)/shard_map/ppermute | solution.py:9
  143.8 1.0 fusion.85
  144.8 3.1 %collective-permute-start.16 = (f32[10,32,128]{2,1,0:T(8,128)S(1)}, f32[10,32,128]{2,1,0:T(8,128)S(1)}, u32[]{:S(2)}, u32[]{:S(2)}) collective-permute-start(f32[10,32,128]{2,1,0:T(8,128)S(1)} %get-tuple-element.159), channel_id=1, source_target_pairs={{0,32},{8,40},{16,48},{24,56},{32,0},{40,8},{48,16},{56,24},{64,96... | collective-permute-start | bytes 491528 | tf_op jit(solution)/shard_map/ppermute | solution.py:9
  148.1 3.4 %collective-permute-start.7 = (f32[2,5,64,128]{3,2,1,0:T(8,128)S(1)}, f32[2,5,64,128]{3,2,1,0:T(8,128)S(1)}, u32[]{:S(2)}, u32[]{:S(2)}) collective-permute-start(f32[2,5,64,128]{3,2,1,0:T(8,128)S(1)} %pad_maximum_fusion.3), channel_id=1, source_target_pairs={{0,8},{8,0},{16,24},{24,16},{32,40},{40,32},{48,56},{56,48},{64,72... | collective-permute-start | bytes 983048 | tf_op jit(solution)/shard_map/ppermute | solution.py:9
  151.5 1.9 collective-permute-start.9
  153.4 13.8 %collective-permute-done.16 = f32[10,32,128]{2,1,0:T(8,128)S(1)} collective-permute-done((f32[10,32,128]{2,1,0:T(8,128)S(1)}, f32[10,32,128]{2,1,0:T(8,128)S(1)}, u32[]{:S(2)}, u32[]{:S(2)}) %collective-permute-start.16) | collective-permute-done | bytes 163872 | tf_op jit(solution)/shard_map/ppermute | solution.py:9
  167.2 1.7 fusion.83
  168.9 2.2 %collective-permute-start.17 = (f32[10,32,128]{2,1,0:T(8,128)}, f32[10,32,128]{2,1,0:T(8,128)}, u32[]{:S(2)}, u32[]{:S(2)}) collective-permute-start(f32[10,32,128]{2,1,0:T(8,128)} %fusion.83), channel_id=1, source_target_pairs={{0,16},{8,24},{16,0},{24,8},{32,48},{40,56},{48,32},{56,40},{64,80... | collective-permute-start | bytes 491528 | tf_op jit(solution)/shard_map/ppermute | solution.py:9
  178.1 1.2 fusion.24
  179.3 18.6 %all-to-all-start.3 = ((f32[8,32,128]{2,1,0:T(8,128)}), f32[8,32,128]{2,1,0:T(8,128)S(1)}, u32[]{:S(2)}, u32[]{:S(2)}) async-start(f32[8,32,128]{2,1,0:T(8,128)} %bitcast.370), calls=%async_computation.3 | async-start | bytes 262144 | tf_op jit(solution)/shard_map/all_to_all | solution.py:19
  198.0 1.0 multiply_add_fusion
  199.0 1.9 collective-permute-start.18
  202.9 1.2 fusion.16
  205.7 1.0 collective-permute-done.18
  206.6 1.1 fusion.63
  209.3 5.3 %all-to-all-start.2 = ((f32[8,32,128]{2,1,0:T(8,128)}), f32[8,32,128]{2,1,0:T(8,128)S(1)}, u32[]{:S(2)}, u32[]{:S(2)}) async-start(f32[8,32,128]{2,1,0:T(8,128)} %bitcast.72), calls=%async_computation.2 | async-start | bytes 262144 | tf_op jit(solution)/shard_map/all_to_all | solution.py:19
  215.2 0.9 copy.36
  216.1 3.7 %all-to-all-done.2 = f32[8,32,128]{2,1,0:T(8,128)S(1)} async-done(((f32[8,32,128]{2,1,0:T(8,128)}), f32[8,32,128]{2,1,0:T(8,128)S(1)}, u32[]{:S(2)}, u32[]{:S(2)}) %all-to-all-start.2) | async-done | bytes 131104 | tf_op jit(solution)/shard_map/all_to_all | solution.py:19
  (254 shorter events, 35.8 us)
Async XLA Ops:
  0.6 23.3 %copy-start = (bf16[256,128]{1,0:T(8,128)(2,1)S(1)}, bf16[256,128]{1,0:T(8,128)(2,1)}, u32[]{:S(2)}) copy-start(bf16[256,128]{1,0:T(8,128)(2,1)} %param.8) | copy-start | bytes 196612
  0.6 23.0 %copy-start.10 = (bf16[256,640]{1,0:T(8,128)(2,1)S(1)}, bf16[256,640]{1,0:T(8,128)(2,1)}, u32[]{:S(2)}) copy-start(bf16[256,640]{1,0:T(8,128)(2,1)} %param.11) | copy-start | bytes 983044
  3.1 36.0 %all-to-all-start = ((f32[16,1,10]{2,1,0:T(1,128)}), f32[16,1,10]{2,1,0:T(1,128)S(1)}, u32[]{:S(2)}, u32[]{:S(2)}) async-start(f32[16,1,10]{2,1,0:T(1,128)} %broadcast_in_dim.258), calls=%async_computation | async-start | bytes 16384 | tf_op jit(solution)/shard_map/all_to_all | solution.py:25
  27.6 34.0 %collective-permute-start = (f32[10,64,128]{2,1,0:T(8,128)}, f32[10,64,128]{2,1,0:T(8,128)S(1)}, u32[]{:S(2)}, u32[]{:S(2)}) collective-permute-start(f32[10,64,128]{2,1,0:T(8,128)} %convolution_bitcast_fusion.9), channel_id=1, source_target_pairs={{0,8},{8,0},{16,24},{24,16},{32,40},{40,32},{48,56},{56,48},{64,72... | collective-permute-start | bytes 983048 | tf_op jit(solution)/shard_map/ppermute | solution.py:9
  30.9 48.4 %collective-permute-start.10 = (f32[3,10,32,128]{3,2,1,0:T(8,128)}, f32[3,10,32,128]{3,2,1,0:T(8,128)}, u32[]{:S(2)}, u32[]{:S(2)}) collective-permute-start(f32[3,10,32,128]{3,2,1,0:T(8,128)} %pad_maximum_fusion), channel_id=1, source_target_pairs={{0,8},{8,0},{16,24},{24,16},{32,40},{40,32},{48,56},{56,48},{64,72... | collective-permute-start | bytes 1474568 | tf_op jit(solution)/shard_map/ppermute | solution.py:9
  39.3 13.6 %copy-start.53 = (f32[10]{0:T(128)}, f32[10]{0:T(128)S(1)}, u32[]{:S(2)}) copy-start(f32[10]{0:T(128)S(1)} %broadcast_select_fusion.10) | copy-start | bytes 124
  39.4 12.6 %copy-start.49 = (f32[10]{0:T(128)}, f32[10]{0:T(128)S(1)}, u32[]{:S(2)}) copy-start(f32[10]{0:T(128)S(1)} %broadcast_select_fusion.12) | copy-start | bytes 124
  39.4 12.5 %copy-start.51 = (f32[10]{0:T(128)}, f32[10]{0:T(128)S(1)}, u32[]{:S(2)}) copy-start(f32[10]{0:T(128)S(1)} %broadcast_select_fusion.14) | copy-start | bytes 124
  39.5 21.5 %copy-start.40 = (f32[10]{0:T(128)}, f32[10]{0:T(128)S(1)}, u32[]{:S(2)}) copy-start(f32[10]{0:T(128)S(1)} %get-tuple-element.112) | copy-start | bytes 124
  44.5 15.8 %all-to-all-start.1 = ((f32[8,1,10]{2,1,0:T(1,128)}), f32[8,1,10]{2,1,0:T(1,128)S(1)}, u32[]{:S(2)}, u32[]{:S(2)}) async-start(f32[8,1,10]{2,1,0:T(1,128)} %broadcast_in_dim.270), calls=%async_computation.1 | async-start | bytes 8192 | tf_op jit(solution)/shard_map/all_to_all | solution.py:25
  54.7 71.0 %collective-permute-start.14 = (f32[3,10,32,128]{3,2,1,0:T(8,128)}, f32[3,10,32,128]{3,2,1,0:T(8,128)}, u32[]{:S(2)}, u32[]{:S(2)}) collective-permute-start(f32[3,10,32,128]{3,2,1,0:T(8,128)} %pad_maximum_fusion.2), channel_id=1, source_target_pairs={{0,8},{8,0},{16,24},{24,16},{32,40},{40,32},{48,56},{56,48},{64,72... | collective-permute-start | bytes 1474568 | tf_op jit(solution)/shard_map/ppermute | solution.py:9
  59.0 146.7 %collective-permute-start.19 = (f32[10,64,128]{2,1,0:T(8,128)}, f32[10,64,128]{2,1,0:T(8,128)}, u32[]{:S(2)}, u32[]{:S(2)}) collective-permute-start(f32[10,64,128]{2,1,0:T(8,128)} %fusion.71), channel_id=1, source_target_pairs={{8,0},{24,16},{40,32},{56,48},{72,64},{88,80},{104,96},{120,112},{... | collective-permute-start | bytes 983048 | tf_op jit(solution)/shard_map/ppermute | solution.py:14
  63.2 8.0 %collective-permute-start.1 = (f32[5,64,128]{2,1,0:T(8,128)}, f32[5,64,128]{2,1,0:T(8,128)S(1)}, u32[]{:S(2)}, u32[]{:S(2)}) collective-permute-start(f32[5,64,128]{2,1,0:T(8,128)} %fusion.97), channel_id=1, source_target_pairs={{0,16},{8,24},{16,0},{24,8},{32,48},{40,56},{48,32},{56,40},{64,80... | collective-permute-start | bytes 491528 | tf_op jit(solution)/shard_map/ppermute | solution.py:9
  72.3 21.4 %copy-start.58 = (f32[10]{0:T(128)S(1)}, f32[10]{0:T(128)}, u32[]{:S(2)}) copy-start(f32[10]{0:T(128)} %copy-done.57) | copy-start | bytes 124
  72.3 15.1 %collective-permute-start.2 = (f32[5,64,128]{2,1,0:T(8,128)S(1)}, f32[5,64,128]{2,1,0:T(8,128)S(1)}, u32[]{:S(2)}, u32[]{:S(2)}) collective-permute-start(f32[5,64,128]{2,1,0:T(8,128)S(1)} %multiply_add_fusion.9), channel_id=1, source_target_pairs={{0,32},{8,40},{16,48},{24,56},{32,0},{40,8},{48,16},{56,24},{64,96... | collective-permute-start | bytes 491528 | tf_op jit(solution)/shard_map/ppermute | solution.py:9
  80.3 22.9 %copy-start.60 = (f32[5]{0:T(128)S(1)}, f32[5]{0:T(128)}, u32[]{:S(2)}) copy-start(f32[5]{0:T(128)} %dynamic_slice.59) | copy-start | bytes 64
  80.3 22.9 %copy-start.61 = (f32[5]{0:T(128)S(1)}, f32[5]{0:T(128)}, u32[]{:S(2)}) copy-start(f32[5]{0:T(128)} %dynamic_slice.60) | copy-start | bytes 64
  80.4 13.4 %collective-permute-start.11 = (f32[10,32,128]{2,1,0:T(8,128)S(1)}, f32[10,32,128]{2,1,0:T(8,128)S(1)}, u32[]{:S(2)}, u32[]{:S(2)}) collective-permute-start(f32[10,32,128]{2,1,0:T(8,128)S(1)} %fusion.96), channel_id=1, source_target_pairs={{0,512},{8,520},{16,528},{24,536},{32,544},{40,552},{48,560},{56,5... | collective-permute-start | bytes 491528 | tf_op jit(solution)/shard_map/ppermute | solution.py:9
  88.2 15.1 %collective-permute-start.3 = (f32[5,64,128]{2,1,0:T(8,128)S(1)}, f32[5,64,128]{2,1,0:T(8,128)S(1)}, u32[]{:S(2)}, u32[]{:S(2)}) collective-permute-start(f32[5,64,128]{2,1,0:T(8,128)S(1)} %multiply_add_fusion.8), channel_id=1, source_target_pairs={{0,64},{8,72},{16,80},{24,88},{32,96},{40,104},{48,112},{56,120},{... | collective-permute-start | bytes 491528 | tf_op jit(solution)/shard_map/ppermute | solution.py:9
  94.8 24.5 %collective-permute-start.12 = (f32[10,32,128]{2,1,0:T(8,128)S(1)}, f32[10,32,128]{2,1,0:T(8,128)S(1)}, u32[]{:S(2)}, u32[]{:S(2)}) collective-permute-start(f32[10,32,128]{2,1,0:T(8,128)S(1)} %fusion.94), channel_id=1, source_target_pairs={{0,256},{8,264},{16,272},{24,280},{32,288},{40,296},{48,304},{56,3... | collective-permute-start | bytes 491528 | tf_op jit(solution)/shard_map/ppermute | solution.py:9
  103.3 20.3 %collective-permute-start.5 = (f32[5,64,128]{2,1,0:T(8,128)S(1)}, f32[5,64,128]{2,1,0:T(8,128)S(1)}, u32[]{:S(2)}, u32[]{:S(2)}) collective-permute-start(f32[5,64,128]{2,1,0:T(8,128)S(1)} %multiply_add_fusion.7), channel_id=1, source_target_pairs={{0,128},{8,136},{16,144},{24,152},{32,160},{40,168},{48,176},{56,1... | collective-permute-start | bytes 491528 | tf_op jit(solution)/shard_map/ppermute | solution.py:9
  105.7 18.0 %copy-start.62 = (f32[5]{0:T(128)S(1)}, f32[5]{0:T(128)}, u32[]{:S(2)}) copy-start(f32[5]{0:T(128)} %dynamic_slice.61) | copy-start | bytes 64
  105.7 18.0 %copy-start.63 = (f32[5]{0:T(128)S(1)}, f32[5]{0:T(128)}, u32[]{:S(2)}) copy-start(f32[5]{0:T(128)} %dynamic_slice.62) | copy-start | bytes 64
  105.7 20.7 %copy-start.54 = (f32[10]{0:T(128)S(1)}, f32[10]{0:T(128)}, u32[]{:S(2)}) copy-start(f32[10]{0:T(128)} %copy-done.53) | copy-start | bytes 124
  105.7 65.5 %collective-permute-start.4 = (f32[3,5,64,128]{3,2,1,0:T(8,128)S(1)}, f32[3,5,64,128]{3,2,1,0:T(8,128)S(1)}, u32[]{:S(2)}, u32[]{:S(2)}) collective-permute-start(f32[3,5,64,128]{3,2,1,0:T(8,128)S(1)} %pad_maximum_fusion.1), channel_id=1, source_target_pairs={{0,8},{8,0},{16,24},{24,16},{32,40},{40,32},{48,56},{56,48},{64,72... | collective-permute-start | bytes 1474568 | tf_op jit(solution)/shard_map/ppermute | solution.py:9
  120.3 6.1 %collective-permute-start.13 = (f32[10,32,128]{2,1,0:T(8,128)S(1)}, f32[10,32,128]{2,1,0:T(8,128)S(1)}, u32[]{:S(2)}, u32[]{:S(2)}) collective-permute-start(f32[10,32,128]{2,1,0:T(8,128)S(1)} %get-tuple-element.161), channel_id=1, source_target_pairs={{0,128},{8,136},{16,144},{24,152},{32,160},{40,168},{48,176},{56,1... | collective-permute-start | bytes 491528 | tf_op jit(solution)/shard_map/ppermute | solution.py:9
  123.8 9.6 %collective-permute-start.6 = (f32[5,64,128]{2,1,0:T(8,128)S(1)}, f32[5,64,128]{2,1,0:T(8,128)S(1)}, u32[]{:S(2)}, u32[]{:S(2)}) collective-permute-start(f32[5,64,128]{2,1,0:T(8,128)S(1)} %multiply_add_fusion.6), channel_id=1, source_target_pairs={{0,256},{8,264},{16,272},{24,280},{32,288},{40,296},{48,304},{56,3... | collective-permute-start | bytes 491528 | tf_op jit(solution)/shard_map/ppermute | solution.py:9
  126.4 17.4 %copy-start.50 = (f32[10]{0:T(128)S(1)}, f32[10]{0:T(128)}, u32[]{:S(2)}) copy-start(f32[10]{0:T(128)} %copy-done.49) | copy-start | bytes 124
  127.4 16.4 %collective-permute-start.15 = (f32[10,32,128]{2,1,0:T(8,128)S(1)}, f32[10,32,128]{2,1,0:T(8,128)S(1)}, u32[]{:S(2)}, u32[]{:S(2)}) collective-permute-start(f32[10,32,128]{2,1,0:T(8,128)S(1)} %fusion.87), channel_id=1, source_target_pairs={{0,64},{8,72},{16,80},{24,88},{32,96},{40,104},{48,112},{56,120},{... | collective-permute-start | bytes 491528 | tf_op jit(solution)/shard_map/ppermute | solution.py:9
  133.5 14.4 %copy-start.9 = (f32[3,10,256]{2,1,0:T(8,128)S(1)}, f32[3,10,256]{2,1,0:T(8,128)}, u32[]{:S(2)}) copy-start(f32[3,10,256]{2,1,0:T(8,128)} %copy-done.8) | copy-start | bytes 92164
  133.5 14.4 %copy-start.41 = (f32[10]{0:T(128)S(1)}, f32[10]{0:T(128)}, u32[]{:S(2)}) copy-start(f32[10]{0:T(128)} %copy-done.40) | copy-start | bytes 124
  133.5 14.4 %copy-start.46 = (f32[10]{0:T(128)S(1)}, f32[10]{0:T(128)}, u32[]{:S(2)}) copy-start(f32[10]{0:T(128)} %get-tuple-element.116) | copy-start | bytes 124
  133.5 14.4 %copy-start.47 = (f32[10]{0:T(128)S(1)}, f32[10]{0:T(128)}, u32[]{:S(2)}) copy-start(f32[10]{0:T(128)} %get-tuple-element.113) | copy-start | bytes 124
  133.5 18.0 %collective-permute-start.8 = (f32[5,64,128]{2,1,0:T(8,128)S(1)}, f32[5,64,128]{2,1,0:T(8,128)S(1)}, u32[]{:S(2)}, u32[]{:S(2)}) collective-permute-start(f32[5,64,128]{2,1,0:T(8,128)S(1)} %multiply_add_fusion.5), channel_id=1, source_target_pairs={{0,512},{8,520},{16,528},{24,536},{32,544},{40,552},{48,560},{56,5... | collective-permute-start | bytes 491528 | tf_op jit(solution)/shard_map/ppermute | solution.py:9
  144.8 22.4 %copy-start.38 = (f32[10]{0:T(128)S(1)}, f32[10]{0:T(128)}, u32[]{:S(2)}) copy-start(f32[10]{0:T(128)} %copy-done.37) | copy-start | bytes 124
  144.8 22.4 %copy-start.52 = (f32[10]{0:T(128)S(1)}, f32[10]{0:T(128)}, u32[]{:S(2)}) copy-start(f32[10]{0:T(128)} %copy-done.51) | copy-start | bytes 124
  144.8 22.4 %collective-permute-start.16 = (f32[10,32,128]{2,1,0:T(8,128)S(1)}, f32[10,32,128]{2,1,0:T(8,128)S(1)}, u32[]{:S(2)}, u32[]{:S(2)}) collective-permute-start(f32[10,32,128]{2,1,0:T(8,128)S(1)} %get-tuple-element.159), channel_id=1, source_target_pairs={{0,32},{8,40},{16,48},{24,56},{32,0},{40,8},{48,16},{56,24},{64,96... | collective-permute-start | bytes 491528 | tf_op jit(solution)/shard_map/ppermute | solution.py:9
  148.1 29.3 %copy-start.16 = (f32[256,10]{0,1:T(8,128)}, f32[256,10]{0,1:T(8,128)S(1)}, u32[]{:S(2)}) copy-start(f32[256,10]{0,1:T(8,128)S(1)} %get-tuple-element.186) | copy-start | bytes 30724
  148.1 27.8 %collective-permute-start.7 = (f32[2,5,64,128]{3,2,1,0:T(8,128)S(1)}, f32[2,5,64,128]{3,2,1,0:T(8,128)S(1)}, u32[]{:S(2)}, u32[]{:S(2)}) collective-permute-start(f32[2,5,64,128]{3,2,1,0:T(8,128)S(1)} %pad_maximum_fusion.3), channel_id=1, source_target_pairs={{0,8},{8,0},{16,24},{24,16},{32,40},{40,32},{48,56},{56,48},{64,72... | collective-permute-start | bytes 983048 | tf_op jit(solution)/shard_map/ppermute | solution.py:9
  151.5 25.1 %collective-permute-start.9 = (f32[1,5,64,128]{3,2,1,0:T(8,128)S(1)}, f32[1,5,64,128]{3,2,1,0:T(8,128)S(1)}, u32[]{:S(2)}, u32[]{:S(2)}) collective-permute-start(f32[1,5,64,128]{3,2,1,0:T(8,128)S(1)} %bitcast.376), channel_id=1, source_target_pairs={{0,8},{8,0},{16,24},{24,16},{32,40},{40,32},{48,56},{56,48},{64,72... | collective-permute-start | bytes 491528 | tf_op jit(solution)/shard_map/ppermute | solution.py:9
  168.9 29.0 %collective-permute-start.17 = (f32[10,32,128]{2,1,0:T(8,128)}, f32[10,32,128]{2,1,0:T(8,128)}, u32[]{:S(2)}, u32[]{:S(2)}) collective-permute-start(f32[10,32,128]{2,1,0:T(8,128)} %fusion.83), channel_id=1, source_target_pairs={{0,16},{8,24},{16,0},{24,8},{32,48},{40,56},{48,32},{56,40},{64,80... | collective-permute-start | bytes 491528 | tf_op jit(solution)/shard_map/ppermute | solution.py:9
  178.1 19.8 %copy-start.2 = (f32[10,32,128]{2,1,0:T(8,128)S(1)}, f32[10,32,128]{2,1,0:T(8,128)}, u32[]{:S(2)}) copy-start(f32[10,32,128]{2,1,0:T(8,128)} %copy-done.1) | copy-start | bytes 491524
  178.1 19.8 %copy-start.39 = (f32[10]{0:T(128)S(1)}, f32[10]{0:T(128)}, u32[]{:S(2)}) copy-start(f32[10]{0:T(128)} %copy-done.37) | copy-start | bytes 124
  178.1 19.8 %copy-start.45 = (f32[10]{0:T(128)S(1)}, f32[10]{0:T(128)}, u32[]{:S(2)}) copy-start(f32[10]{0:T(128)} %copy-done.44) | copy-start | bytes 124
  179.3 21.6 %copy-start.17 = (f32[256,10]{0,1:T(8,128)S(1)}, f32[256,10]{0,1:T(8,128)}, u32[]{:S(2)}) copy-start(f32[256,10]{0,1:T(8,128)} %copy-done.16) | copy-start | bytes 30724
  179.3 25.7 %all-to-all-start.3 = ((f32[8,32,128]{2,1,0:T(8,128)}), f32[8,32,128]{2,1,0:T(8,128)S(1)}, u32[]{:S(2)}, u32[]{:S(2)}) async-start(f32[8,32,128]{2,1,0:T(8,128)} %bitcast.370), calls=%async_computation.3 | async-start | bytes 262144 | tf_op jit(solution)/shard_map/all_to_all | solution.py:19
  199.0 7.6 %collective-permute-start.18 = (f32[10,32,128]{2,1,0:T(8,128)S(1)}, f32[10,32,128]{2,1,0:T(8,128)S(1)}, u32[]{:S(2)}, u32[]{:S(2)}) collective-permute-start(f32[10,32,128]{2,1,0:T(8,128)S(1)} %multiply_add_fusion), channel_id=1, source_target_pairs={{0,8},{8,0},{16,24},{24,16},{32,40},{40,32},{48,56},{56,48},{64,72... | collective-permute-start | bytes 491528 | tf_op jit(solution)/shard_map/ppermute | solution.py:9
  209.3 10.5 %all-to-all-start.2 = ((f32[8,32,128]{2,1,0:T(8,128)}), f32[8,32,128]{2,1,0:T(8,128)S(1)}, u32[]{:S(2)}, u32[]{:S(2)}) async-start(f32[8,32,128]{2,1,0:T(8,128)} %bitcast.72), calls=%async_computation.2 | async-start | bytes 262144 | tf_op jit(solution)/shard_map/all_to_all | solution.py:19
  (40 other events, 130.8 us)

commit v3 on v2

--- a/solution.py
+++ b/solution.py
@@ -123,20 +123,15 @@
         return keep, pull
 
     z_levels, z_prefix = sibling_spans(z_spans, z_place)
-    member = jnp.arange(ring)
-    own_reach = jnp.exp(sum_where(member < z_place, z_spans))
-    peer_reach = jnp.exp(sum_where(member < (z_place ^ 1), z_spans))
     row_total = jnp.sum(z_spans, axis=0)
-    z_factors, z_offsets, z_prefix, reaches, row_total = lax.optimization_barrier(
+    z_factors, z_offsets, z_prefix, row_total = lax.optimization_barrier(
         (
             factors(z_levels, 0),
             [level[2] for level in z_levels],
             z_prefix,
-            (own_reach, peer_reach),
             row_total,
         )
     )
-    own_reach, peer_reach = (reach[:, None, None] for reach in reaches)
     y_spans = all_totals(row_total, along_y)
     y_levels, _ = sibling_spans(y_spans, y_place)
     offsets = z_offsets + [z_prefix + level[2] for level in y_levels]
@@ -157,15 +152,11 @@
     def bucket_grad(part):
         return jnp.einsum("thp,tn->hpn", part, state_read, preferred_element_type=jnp.float32)
 
-    near, far = (range(1, Z_BITS), range(Z_BITS, level_count))
-    start = lax.optimization_barrier((running, scaled[Z_BITS + 1 :], shard_index))
-    early_grads = {
-        bit: bucket_grad(weigh(coefficient(start[1][bit - Z_BITS], start[0], bit, start[2])))
-        for bit in far
-    }
-    early_sent = jnp.stack([other_half(early_grads[bit], start[2] % 2) for bit in far])
+    far = range(Z_BITS, level_count)
     coefficients, weighted = ([], [])
-    *start, state, early_sent = lax.optimization_barrier((*start, state, early_sent))
+    *start, state = lax.optimization_barrier(
+        (running, scaled[Z_BITS + 1 :], shard_index, state)
+    )
     for bit in range(Z_BITS):
         log_reach = start[0] + offsets[bit][:, None] if bit else start[0]
         coefficients.append(coefficient(scaled[bit + 1], log_reach, bit, start[2]))
@@ -178,6 +169,7 @@
         log_reach = start[0] + row_offsets[bit - Z_BITS][:, None]
         coefficients.append(coefficient(start[1][bit - Z_BITS], log_reach, bit, start[2]))
         weighted.append(weigh(coefficients[bit]))
+        level_grads.append(bucket_grad(weighted[bit]))
     buckets = {0: exchange(state, 0)}
     half_state = up.mine(up.join(0, state, buckets[0]))
     half_buckets = {}
@@ -190,23 +182,14 @@
             buckets[bit] = up.whole(half_buckets[bit], others[place])
     first_grads = to_left(level_grads[0])
     half_grads = {}
-    others = exchange(jnp.stack([down.theirs(level_grads[bit]) for bit in near]), 0)
-    for place, bit in enumerate(near):
-        half_grads[bit] = down.mine(level_grads[bit]) + others[place]
-    others = exchange(early_sent, 0)
-    y_member = jnp.arange(rows)
-    for place, bit in enumerate(far):
-        half_grads[bit] = own_reach * down.mine(early_grads[bit]) + peer_reach * others[place]
-    top = level_count - 1
-    sender = y_place ^ (rows // 2)
-    before = (y_member >= sender // (rows // 2) * (rows // 2)) & (y_member < sender)
-    row_reach = jnp.exp(sum_where(before, y_spans))[:, None, None]
-    half_carried = row_reach * exchange(half_grads[top], top)
-    for bit in reversed(range(1, top)):
-        grad = half_grads[bit]
-        if bit >= Z_BITS:
-            grad = jnp.exp(y_levels[bit - Z_BITS][2])[:, None, None] * grad
-        incoming = exchange(grad + down.pull[bit] * half_carried, bit)
+    for bits in GATHERS:
+        sent = jnp.stack([down.theirs(level_grads[bit]) for bit in bits])
+        others = exchange(sent, 0)
+        for place, bit in enumerate(bits):
+            half_grads[bit] = down.mine(level_grads[bit]) + others[place]
+    half_carried = jnp.zeros_like(half_grads[1])
+    for bit in reversed(range(1, level_count)):
+        incoming = exchange(half_grads[bit] + down.pull[bit] * half_carried, bit)
         half_carried = down.keep[bit] * half_carried + incoming
     pair_grad = down.whole(half_carried, exchange(half_carried, 0))
     dstate = down.keep[0] * pair_grad + first_grads

time: 225 us -> 223 us (level); the launches traced: 220 us -> 221 us
  waiting for transfers between devices: 29.7 us -> 48.2 us
  starting transfers between devices: 133 us -> 121 us
  other arithmetic: 23.2 us -> 14.3 us
    ppermute x19 -> x20, waiting for transfers between devices: 25.9 us -> 43.1 us  [exchange(): return lax.ppermute(value, 'ctx', pairs)]
    ppermute x19 -> x20, starting transfers between devices: 81.3 us -> 70.7 us  [exchange(): return lax.ppermute(value, 'ctx', pairs)]
    add x6, other arithmetic: 6.86 us -> 3.34 us  [mixer(): incoming = exchange(half_grads[bit] + down.pull[bit] * half_carried, bit)]
    unnamed x134 -> x130, local copies, waits for them, and re-layouts: 5.36 us -> 5.3 us
  transfers between devices with their start and end apart: 24 -> 25, of which waited for: 7 -> 11; matrix products, arithmetic and copies ran while one was open for 21% -> 18% of each run, Pallas kernels for 0% -> 0%
where the time goes in v3:
time: 223 us; the launch traced here: 221 us
  starting transfers between devices  121 us (54%)
  waiting for transfers between devices  48.2 us (22%)
  matrix products  18.8 us (8%)
  local copies, waits for them, and re-layouts  16.3 us (7%)
  other arithmetic  14.3 us (6%)
  between operations  2.78 us (1%)
    ppermute x20, starting transfers between devices, exchange(): return lax.ppermute(value, 'ctx', pairs)  70.7 us
    ppermute x20, waiting for transfers between devices, exchange(): return lax.ppermute(value, 'ctx', pairs)  43.1 us
    all_to_all x2, starting transfers between devices, all_totals(): lax.all_to_all(mine, 'ctx', 0, 0, axis_index_groups=groups, tiled=True)  26.2 us
    all_to_all x2, starting transfers between devices, sum_at_owner(): lax.all_to_all(pieces, axis, split_axis=0, concat_axis=0, tiled=True)  22.7 us
    dynamic_slice x12, local copies, waits for them, and re-layouts, part(): return lax.dynamic_slice_in_dim(value, place * half, half, axis=0)  7.53 us
    dot_general x7, matrix products, mixer(): jnp.einsum('thp,hpn->tn', weighted[bit].astype(jnp.float32), buckets[bit]...  6.34 us
    unnamed x130, local copies, waits for them, and re-layouts  5.3 us
    all_to_all x2, waiting for transfers between devices, sum_at_owner(): lax.all_to_all(pieces, axis, split_axis=0, concat_axis=0, tiled=True)  4.92 us
  transfers between devices with their start and end apart: 25, of which 11 were waited for; matrix products, arithmetic and copies ran while one was open for 18% of the time, Pallas kernels for 0%

profile of v3, /device:TPU:1, one launch (start us, length us, event | category | flops | bytes accessed | tf_op | source)
XLA Modules:
  0.0 221.4 jit_solution(136888544777922061)
XLA Ops:
  3.1 19.4 %all-to-all-start = ((f32[16,1,10]{2,1,0:T(1,128)}), f32[16,1,10]{2,1,0:T(1,128)S(1)}, u32[]{:S(2)}, u32[]{:S(2)}) async-start(f32[16,1,10]{2,1,0:T(1,128)} %broadcast_in_dim.233), calls=%async_computation | async-start | bytes 16384 | tf_op jit(solution)/shard_map/all_to_all | solution.py:25
  22.6 1.1 copy.32
  23.9 1.3 convolution_bitcast_fusion.9
  25.2 3.3 %collective-permute-start = (f32[10,64,128]{2,1,0:T(8,128)}, f32[10,64,128]{2,1,0:T(8,128)S(1)}, u32[]{:S(2)}, u32[]{:S(2)}) collective-permute-start(f32[10,64,128]{2,1,0:T(8,128)} %convolution_bitcast_fusion.9), channel_id=1, source_target_pairs={{0,8},{8,0},{16,24},{24,16},{32,40},{40,32},{48,56},{56,48},{64,72... | collective-permute-start | bytes 983048 | tf_op jit(solution)/shard_map/ppermute | solution.py:9
  29.9 1.3 convert_reduce_fusion
  32.5 1.0 fusion.25
  39.0 6.8 %all-to-all-start.1 = ((f32[8,1,10]{2,1,0:T(1,128)}), f32[8,1,10]{2,1,0:T(1,128)S(1)}, u32[]{:S(2)}, u32[]{:S(2)}) async-start(f32[8,1,10]{2,1,0:T(1,128)} %broadcast_in_dim.243), calls=%async_computation.1 | async-start | bytes 8192 | tf_op jit(solution)/shard_map/all_to_all | solution.py:25
  49.0 2.3 %collective-permute-start.15 = (f32[3,10,32,128]{3,2,1,0:T(8,128)}, f32[3,10,32,128]{3,2,1,0:T(8,128)}, u32[]{:S(2)}, u32[]{:S(2)}) collective-permute-start(f32[3,10,32,128]{3,2,1,0:T(8,128)} %pad_maximum_fusion.1), channel_id=1, source_target_pairs={{0,8},{8,0},{16,24},{24,16},{32,40},{40,32},{48,56},{56,48},{64,72... | collective-permute-start | bytes 1474568 | tf_op jit(solution)/shard_map/ppermute | solution.py:9
  51.3 1.0 fusion.53
  52.3 1.3 collective-permute-start.20
  57.3 4.7 %collective-permute-start.10 = (f32[1,10,32,128]{3,2,1,0:T(8,128)S(1)}, f32[1,10,32,128]{3,2,1,0:T(8,128)S(1)}, u32[]{:S(2)}, u32[]{:S(2)}) collective-permute-start(f32[1,10,32,128]{3,2,1,0:T(8,128)S(1)} %select_bitcast_fusion.5), channel_id=1, source_target_pairs={{0,8},{8,0},{16,24},{24,16},{32,40},{40,32},{48,56},{56,48},{64,72... | collective-permute-start | bytes 491528 | tf_op jit(solution)/shard_map/ppermute | solution.py:9
  62.7 1.9 collective-permute-start.12
  64.7 7.5 %collective-permute-done.10 = f32[1,10,32,128]{3,2,1,0:T(8,128)S(1)} collective-permute-done((f32[1,10,32,128]{3,2,1,0:T(8,128)S(1)}, f32[1,10,32,128]{3,2,1,0:T(8,128)S(1)}, u32[]{:S(2)}, u32[]{:S(2)}) %collective-permute-start.10) | collective-permute-done | bytes 163872 | tf_op jit(solution)/shard_map/ppermute | solution.py:9
  72.3 7.0 %collective-permute-start.11 = (f32[10,32,128]{2,1,0:T(8,128)S(1)}, f32[10,32,128]{2,1,0:T(8,128)S(1)}, u32[]{:S(2)}, u32[]{:S(2)}) collective-permute-start(f32[10,32,128]{2,1,0:T(8,128)S(1)} %fusion.84), channel_id=1, source_target_pairs={{0,512},{8,520},{16,528},{24,536},{32,544},{40,552},{48,560},{56,5... | collective-permute-start | bytes 491528 | tf_op jit(solution)/shard_map/ppermute | solution.py:9
  79.3 1.0 fusion.83
  80.4 4.5 %collective-permute-start.1 = (f32[5,64,128]{2,1,0:T(8,128)S(1)}, f32[5,64,128]{2,1,0:T(8,128)S(1)}, u32[]{:S(2)}, u32[]{:S(2)}) collective-permute-start(f32[5,64,128]{2,1,0:T(8,128)S(1)} %fusion.83), channel_id=1, source_target_pairs={{0,16},{8,24},{16,0},{24,8},{32,48},{40,56},{48,32},{56,40},{64,80... | collective-permute-start | bytes 491528 | tf_op jit(solution)/shard_map/ppermute | solution.py:9
  85.0 3.1 %collective-permute-start.13 = (f32[10,32,128]{2,1,0:T(8,128)S(1)}, f32[10,32,128]{2,1,0:T(8,128)S(1)}, u32[]{:S(2)}, u32[]{:S(2)}) collective-permute-start(f32[10,32,128]{2,1,0:T(8,128)S(1)} %fusion.82), channel_id=1, source_target_pairs={{0,256},{8,264},{16,272},{24,280},{32,288},{40,296},{48,304},{56,3... | collective-permute-start | bytes 491528 | tf_op jit(solution)/shard_map/ppermute | solution.py:9
  88.6 7.2 %collective-permute-start.2 = (f32[5,64,128]{2,1,0:T(8,128)S(1)}, f32[5,64,128]{2,1,0:T(8,128)S(1)}, u32[]{:S(2)}, u32[]{:S(2)}) collective-permute-start(f32[5,64,128]{2,1,0:T(8,128)S(1)} %multiply_add_fusion.9), channel_id=1, source_target_pairs={{0,32},{8,40},{16,48},{24,56},{32,0},{40,8},{48,16},{56,24},{64,96... | collective-permute-start | bytes 491528 | tf_op jit(solution)/shard_map/ppermute | solution.py:9
  96.0 2.3 %collective-permute-start.14 = (f32[10,32,128]{2,1,0:T(8,128)S(1)}, f32[10,32,128]{2,1,0:T(8,128)S(1)}, u32[]{:S(2)}, u32[]{:S(2)}) collective-permute-start(f32[10,32,128]{2,1,0:T(8,128)S(1)} %get-tuple-element.148), channel_id=1, source_target_pairs={{0,128},{8,136},{16,144},{24,152},{32,160},{40,168},{48,176},{56,1... | collective-permute-start | bytes 491528 | tf_op jit(solution)/shard_map/ppermute | solution.py:9
  98.3 3.9 %collective-permute-done.2 = f32[5,64,128]{2,1,0:T(8,128)S(1)} collective-permute-done((f32[5,64,128]{2,1,0:T(8,128)S(1)}, f32[5,64,128]{2,1,0:T(8,128)S(1)}, u32[]{:S(2)}, u32[]{:S(2)}) %collective-permute-start.2) | collective-permute-done | bytes 163872 | tf_op jit(solution)/shard_map/ppermute | solution.py:9
  102.3 11.6 %collective-permute-start.3 = (f32[5,64,128]{2,1,0:T(8,128)S(1)}, f32[5,64,128]{2,1,0:T(8,128)S(1)}, u32[]{:S(2)}, u32[]{:S(2)}) collective-permute-start(f32[5,64,128]{2,1,0:T(8,128)S(1)} %multiply_add_fusion.8), channel_id=1, source_target_pairs={{0,64},{8,72},{16,80},{24,88},{32,96},{40,104},{48,112},{56,120},{... | collective-permute-start | bytes 491528 | tf_op jit(solution)/shard_map/ppermute | solution.py:9
  114.0 1.0 fusion.78
  115.0 2.4 %collective-permute-start.16 = (f32[10,32,128]{2,1,0:T(8,128)S(1)}, f32[10,32,128]{2,1,0:T(8,128)S(1)}, u32[]{:S(2)}, u32[]{:S(2)}) collective-permute-start(f32[10,32,128]{2,1,0:T(8,128)S(1)} %fusion.78), channel_id=1, source_target_pairs={{0,64},{8,72},{16,80},{24,88},{32,96},{40,104},{48,112},{56,120},{... | collective-permute-start | bytes 491528 | tf_op jit(solution)/shard_map/ppermute | solution.py:9
  118.1 2.1 collective-permute-start.5
  120.3 1.9 collective-permute-start.4
  122.3 23.7 %collective-permute-done.16 = f32[10,32,128]{2,1,0:T(8,128)S(1)} collective-permute-done((f32[10,32,128]{2,1,0:T(8,128)S(1)}, f32[10,32,128]{2,1,0:T(8,128)S(1)}, u32[]{:S(2)}, u32[]{:S(2)}) %collective-permute-start.16) | collective-permute-done | bytes 163872 | tf_op jit(solution)/shard_map/ppermute | solution.py:9
  145.9 1.0 fusion.76
  147.0 1.9 collective-permute-start.17
  149.0 1.9 collective-permute-start.6
  151.0 6.1 %collective-permute-done.17 = f32[10,32,128]{2,1,0:T(8,128)S(1)} collective-permute-done((f32[10,32,128]{2,1,0:T(8,128)S(1)}, f32[10,32,128]{2,1,0:T(8,128)S(1)}, u32[]{:S(2)}, u32[]{:S(2)}) %collective-permute-start.17) | collective-permute-done | bytes 163872 | tf_op jit(solution)/shard_map/ppermute | solution.py:9
  157.1 1.0 fusion.74
  158.1 1.9 collective-permute-start.18
  160.2 3.5 %collective-permute-start.8 = (f32[5,64,128]{2,1,0:T(8,128)S(1)}, f32[5,64,128]{2,1,0:T(8,128)}, u32[]{:S(2)}, u32[]{:S(2)}) collective-permute-start(f32[5,64,128]{2,1,0:T(8,128)S(1)} %multiply_add_fusion.5), channel_id=1, source_target_pairs={{0,512},{8,520},{16,528},{24,536},{32,544},{40,552},{48,560},{56,5... | collective-permute-start | bytes 491528 | tf_op jit(solution)/shard_map/ppermute | solution.py:9
  164.4 1.9 collective-permute-start.7
  166.9 2.9 %collective-permute-start.19 = (f32[10,32,128]{2,1,0:T(8,128)S(1)}, f32[10,32,128]{2,1,0:T(8,128)S(1)}, u32[]{:S(2)}, u32[]{:S(2)}) collective-permute-start(f32[10,32,128]{2,1,0:T(8,128)S(1)} %multiply_add_fusion), channel_id=1, source_target_pairs={{0,8},{8,0},{16,24},{24,16},{32,40},{40,32},{48,56},{56,48},{64,72... | collective-permute-start | bytes 491528 | tf_op jit(solution)/shard_map/ppermute | solution.py:9
  170.3 2.2 %collective-permute-start.9 = (f32[1,5,64,128]{3,2,1,0:T(8,128)}, f32[1,5,64,128]{3,2,1,0:T(8,128)}, u32[]{:S(2)}, u32[]{:S(2)}) collective-permute-start(f32[1,5,64,128]{3,2,1,0:T(8,128)} %bitcast.43), channel_id=1, source_target_pairs={{0,8},{8,0},{16,24},{24,16},{32,40},{40,32},{48,56},{56,48},{64,72... | collective-permute-start | bytes 491528 | tf_op jit(solution)/shard_map/ppermute | solution.py:9
  175.5 1.2 convolution_bitcast_fusion.13
  176.7 1.2 convolution_bitcast_fusion.15
  177.9 1.2 convolution_bitcast_fusion.14
  179.1 1.1 fusion.51
  181.4 18.5 %all-to-all-start.2 = ((f32[8,32,128]{2,1,0:T(8,128)}), f32[8,32,128]{2,1,0:T(8,128)S(1)}, u32[]{:S(2)}, u32[]{:S(2)}) async-start(f32[8,32,128]{2,1,0:T(8,128)} %bitcast.66), calls=%async_computation.2 | async-start | bytes 262144 | tf_op jit(solution)/shard_map/all_to_all | solution.py:19
  201.4 3.8 %all-to-all-done.2 = f32[8,32,128]{2,1,0:T(8,128)S(1)} async-done(((f32[8,32,128]{2,1,0:T(8,128)}), f32[8,32,128]{2,1,0:T(8,128)S(1)}, u32[]{:S(2)}, u32[]{:S(2)}) %all-to-all-start.2) | async-done | bytes 131104 | tf_op jit(solution)/shard_map/all_to_all | solution.py:19
  205.8 1.1 fusion.38
  207.4 1.0 slice_bitcast_fusion.5
  210.2 1.2 fusion.24
  211.3 4.1 %all-to-all-start.3 = ((f32[8,32,128]{2,1,0:T(8,128)}), f32[8,32,128]{2,1,0:T(8,128)S(1)}, u32[]{:S(2)}, u32[]{:S(2)}) async-start(f32[8,32,128]{2,1,0:T(8,128)} %bitcast.74), calls=%async_computation.3 | async-start | bytes 262144 | tf_op jit(solution)/shard_map/all_to_all | solution.py:19
  217.4 1.2 fusion.16
  219.6 1.2 all-to-all-done.3
  (254 shorter events, 32.7 us)
Async XLA Ops:
  0.6 31.3 %copy-start = (bf16[256,128]{1,0:T(8,128)(2,1)S(1)}, bf16[256,128]{1,0:T(8,128)(2,1)}, u32[]{:S(2)}) copy-start(bf16[256,128]{1,0:T(8,128)(2,1)} %param.8) | copy-start | bytes 196612
  0.6 23.2 %copy-start.1 = (bf16[256,128]{1,0:T(8,128)(2,1)S(1)}, bf16[256,128]{1,0:T(8,128)(2,1)}, u32[]{:S(2)}) copy-start(bf16[256,128]{1,0:T(8,128)(2,1)} %param.7) | copy-start | bytes 196612
  0.7 23.2 %copy-start.15 = (s32[8,10,256]{2,0,1:T(8,128)S(1)}, s32[8,10,256]{2,0,1:T(8,128)}, u32[]{:S(2)}) copy-start(s32[8,10,256]{2,0,1:T(8,128)} %param.10) | copy-start | bytes 245764
  3.1 30.7 %all-to-all-start = ((f32[16,1,10]{2,1,0:T(1,128)}), f32[16,1,10]{2,1,0:T(1,128)S(1)}, u32[]{:S(2)}, u32[]{:S(2)}) async-start(f32[16,1,10]{2,1,0:T(1,128)} %broadcast_in_dim.233), calls=%async_computation | async-start | bytes 16384 | tf_op jit(solution)/shard_map/all_to_all | solution.py:25
  23.9 22.6 %copy-start.2 = (f32[8,10,256]{2,1,0:T(8,128)}, f32[8,10,256]{2,1,0:T(8,128)S(1)}, u32[]{:S(2)}) copy-start(f32[8,10,256]{2,1,0:T(8,128)S(1)} %fusion.85) | copy-start | bytes 245764
  25.2 54.1 %collective-permute-start = (f32[10,64,128]{2,1,0:T(8,128)}, f32[10,64,128]{2,1,0:T(8,128)S(1)}, u32[]{:S(2)}, u32[]{:S(2)}) collective-permute-start(f32[10,64,128]{2,1,0:T(8,128)} %convolution_bitcast_fusion.9), channel_id=1, source_target_pairs={{0,8},{8,0},{16,24},{24,16},{32,40},{40,32},{48,56},{56,48},{64,72... | collective-permute-start | bytes 983048 | tf_op jit(solution)/shard_map/ppermute | solution.py:9
  33.9 13.8 %copy-start.43 = (f32[10]{0:T(128)}, f32[10]{0:T(128)S(1)}, u32[]{:S(2)}) copy-start(f32[10]{0:T(128)S(1)} %broadcast_select_fusion.12) | copy-start | bytes 124
  39.0 14.6 %all-to-all-start.1 = ((f32[8,1,10]{2,1,0:T(1,128)}), f32[8,1,10]{2,1,0:T(1,128)S(1)}, u32[]{:S(2)}, u32[]{:S(2)}) async-start(f32[8,1,10]{2,1,0:T(1,128)} %broadcast_in_dim.243), calls=%async_computation.1 | async-start | bytes 8192 | tf_op jit(solution)/shard_map/all_to_all | solution.py:25
  49.0 64.9 %collective-permute-start.15 = (f32[3,10,32,128]{3,2,1,0:T(8,128)}, f32[3,10,32,128]{3,2,1,0:T(8,128)}, u32[]{:S(2)}, u32[]{:S(2)}) collective-permute-start(f32[3,10,32,128]{3,2,1,0:T(8,128)} %pad_maximum_fusion.1), channel_id=1, source_target_pairs={{0,8},{8,0},{16,24},{24,16},{32,40},{40,32},{48,56},{56,48},{64,72... | collective-permute-start | bytes 1474568 | tf_op jit(solution)/shard_map/ppermute | solution.py:9
  52.3 126.8 %collective-permute-start.20 = (f32[10,64,128]{2,1,0:T(8,128)}, f32[10,64,128]{2,1,0:T(8,128)}, u32[]{:S(2)}, u32[]{:S(2)}) collective-permute-start(f32[10,64,128]{2,1,0:T(8,128)} %fusion.53), channel_id=1, source_target_pairs={{8,0},{24,16},{40,32},{56,48},{72,64},{88,80},{104,96},{120,112},{... | collective-permute-start | bytes 983048 | tf_op jit(solution)/shard_map/ppermute | solution.py:14
  57.3 14.8 %collective-permute-start.10 = (f32[1,10,32,128]{3,2,1,0:T(8,128)S(1)}, f32[1,10,32,128]{3,2,1,0:T(8,128)S(1)}, u32[]{:S(2)}, u32[]{:S(2)}) collective-permute-start(f32[1,10,32,128]{3,2,1,0:T(8,128)S(1)} %select_bitcast_fusion.5), channel_id=1, source_target_pairs={{0,8},{8,0},{16,24},{24,16},{32,40},{40,32},{48,56},{56,48},{64,72... | collective-permute-start | bytes 491528 | tf_op jit(solution)/shard_map/ppermute | solution.py:9
  62.6 16.6 %copy-start.45 = (f32[5]{0:T(128)S(1)}, f32[5]{0:T(128)}, u32[]{:S(2)}) copy-start(f32[5]{0:T(128)} %dynamic-slice.10) | copy-start | bytes 64
  62.7 16.6 %copy-start.46 = (f32[5]{0:T(128)S(1)}, f32[5]{0:T(128)}, u32[]{:S(2)}) copy-start(f32[5]{0:T(128)} %dynamic-slice.11) | copy-start | bytes 64
  62.7 22.2 %copy-start.60 = (f32[10]{0:T(128)S(1)}, f32[10]{0:T(128)}, u32[]{:S(2)}) copy-start(f32[10]{0:T(128)} %copy-done.59) | copy-start | bytes 124
  62.7 22.1 %collective-permute-start.12 = (f32[2,10,32,128]{3,2,1,0:T(8,128)S(1)}, f32[2,10,32,128]{3,2,1,0:T(8,128)S(1)}, u32[]{:S(2)}, u32[]{:S(2)}) collective-permute-start(f32[2,10,32,128]{3,2,1,0:T(8,128)S(1)} %pad_maximum_fusion.3), channel_id=1, source_target_pairs={{0,8},{8,0},{16,24},{24,16},{32,40},{40,32},{48,56},{56,48},{64,72... | collective-permute-start | bytes 983048 | tf_op jit(solution)/shard_map/ppermute | solution.py:9
  72.3 16.2 %copy-start.53 = (f32[5]{0:T(128)S(1)}, f32[5]{0:T(128)}, u32[]{:S(2)}) copy-start(f32[5]{0:T(128)} %dynamic_slice.52) | copy-start | bytes 64
  72.3 16.2 %copy-start.54 = (f32[5]{0:T(128)S(1)}, f32[5]{0:T(128)}, u32[]{:S(2)}) copy-start(f32[5]{0:T(128)} %dynamic_slice.53) | copy-start | bytes 64
  72.3 12.6 %collective-permute-start.11 = (f32[10,32,128]{2,1,0:T(8,128)S(1)}, f32[10,32,128]{2,1,0:T(8,128)S(1)}, u32[]{:S(2)}, u32[]{:S(2)}) collective-permute-start(f32[10,32,128]{2,1,0:T(8,128)S(1)} %fusion.84), channel_id=1, source_target_pairs={{0,512},{8,520},{16,528},{24,536},{32,544},{40,552},{48,560},{56,5... | collective-permute-start | bytes 491528 | tf_op jit(solution)/shard_map/ppermute | solution.py:9
  80.3 15.5 %copy-start.38 = (f32[10]{0:T(128)S(1)}, f32[10]{0:T(128)}, u32[]{:S(2)}) copy-start(f32[10]{0:T(128)} %copy-done.37) | copy-start | bytes 124
  80.3 15.5 %copy-start.48 = (f32[10]{0:T(128)S(1)}, f32[10]{0:T(128)}, u32[]{:S(2)}) copy-start(f32[10]{0:T(128)} %copy-done.47) | copy-start | bytes 124
  80.4 8.1 %collective-permute-start.1 = (f32[5,64,128]{2,1,0:T(8,128)S(1)}, f32[5,64,128]{2,1,0:T(8,128)S(1)}, u32[]{:S(2)}, u32[]{:S(2)}) collective-permute-start(f32[5,64,128]{2,1,0:T(8,128)S(1)} %fusion.83), channel_id=1, source_target_pairs={{0,16},{8,24},{16,0},{24,8},{32,48},{40,56},{48,32},{56,40},{64,80... | collective-permute-start | bytes 491528 | tf_op jit(solution)/shard_map/ppermute | solution.py:9
  85.0 10.8 %collective-permute-start.13 = (f32[10,32,128]{2,1,0:T(8,128)S(1)}, f32[10,32,128]{2,1,0:T(8,128)S(1)}, u32[]{:S(2)}, u32[]{:S(2)}) collective-permute-start(f32[10,32,128]{2,1,0:T(8,128)S(1)} %fusion.82), channel_id=1, source_target_pairs={{0,256},{8,264},{16,272},{24,280},{32,288},{40,296},{48,304},{56,3... | collective-permute-start | bytes 491528 | tf_op jit(solution)/shard_map/ppermute | solution.py:9
  88.6 25.4 %copy-start.28 = (f32[10]{0:T(128)S(1)}, f32[10]{0:T(128)}, u32[]{:S(2)}) copy-start(f32[10]{0:T(128)} %copy-done.27) | copy-start | bytes 124
  88.6 25.4 %copy-start.44 = (f32[10]{0:T(128)S(1)}, f32[10]{0:T(128)}, u32[]{:S(2)}) copy-start(f32[10]{0:T(128)} %copy-done.43) | copy-start | bytes 124
  88.6 13.6 %collective-permute-start.2 = (f32[5,64,128]{2,1,0:T(8,128)S(1)}, f32[5,64,128]{2,1,0:T(8,128)S(1)}, u32[]{:S(2)}, u32[]{:S(2)}) collective-permute-start(f32[5,64,128]{2,1,0:T(8,128)S(1)} %multiply_add_fusion.9), channel_id=1, source_target_pairs={{0,32},{8,40},{16,48},{24,56},{32,0},{40,8},{48,16},{56,24},{64,96... | collective-permute-start | bytes 491528 | tf_op jit(solution)/shard_map/ppermute | solution.py:9
  95.9 22.1 %copy-start.49 = (f32[5]{0:T(128)S(1)}, f32[5]{0:T(128)}, u32[]{:S(2)}) copy-start(f32[5]{0:T(128)} %dynamic_slice.59) | copy-start | bytes 64
  95.9 22.1 %copy-start.50 = (f32[5]{0:T(128)S(1)}, f32[5]{0:T(128)}, u32[]{:S(2)}) copy-start(f32[5]{0:T(128)} %dynamic_slice.60) | copy-start | bytes 64
  96.0 18.0 %collective-permute-start.14 = (f32[10,32,128]{2,1,0:T(8,128)S(1)}, f32[10,32,128]{2,1,0:T(8,128)S(1)}, u32[]{:S(2)}, u32[]{:S(2)}) collective-permute-start(f32[10,32,128]{2,1,0:T(8,128)S(1)} %get-tuple-element.148), channel_id=1, source_target_pairs={{0,128},{8,136},{16,144},{24,152},{32,160},{40,168},{48,176},{56,1... | collective-permute-start | bytes 491528 | tf_op jit(solution)/shard_map/ppermute | solution.py:9
  102.3 15.8 %collective-permute-start.3 = (f32[5,64,128]{2,1,0:T(8,128)S(1)}, f32[5,64,128]{2,1,0:T(8,128)S(1)}, u32[]{:S(2)}, u32[]{:S(2)}) collective-permute-start(f32[5,64,128]{2,1,0:T(8,128)S(1)} %multiply_add_fusion.8), channel_id=1, source_target_pairs={{0,64},{8,72},{16,80},{24,88},{32,96},{40,104},{48,112},{56,120},{... | collective-permute-start | bytes 491528 | tf_op jit(solution)/shard_map/ppermute | solution.py:9
  115.0 31.0 %copy-start.32 = (f32[10]{0:T(128)S(1)}, f32[10]{0:T(128)}, u32[]{:S(2)}) copy-start(f32[10]{0:T(128)} %copy-done.31) | copy-start | bytes 124
  115.0 31.0 %copy-start.40 = (f32[10]{0:T(128)S(1)}, f32[10]{0:T(128)}, u32[]{:S(2)}) copy-start(f32[10]{0:T(128)} %copy-done.39) | copy-start | bytes 124
  115.0 30.9 %collective-permute-start.16 = (f32[10,32,128]{2,1,0:T(8,128)S(1)}, f32[10,32,128]{2,1,0:T(8,128)S(1)}, u32[]{:S(2)}, u32[]{:S(2)}) collective-permute-start(f32[10,32,128]{2,1,0:T(8,128)S(1)} %fusion.78), channel_id=1, source_target_pairs={{0,64},{8,72},{16,80},{24,88},{32,96},{40,104},{48,112},{56,120},{... | collective-permute-start | bytes 491528 | tf_op jit(solution)/shard_map/ppermute | solution.py:9
  118.1 30.8 %collective-permute-start.5 = (f32[5,64,128]{2,1,0:T(8,128)S(1)}, f32[5,64,128]{2,1,0:T(8,128)S(1)}, u32[]{:S(2)}, u32[]{:S(2)}) collective-permute-start(f32[5,64,128]{2,1,0:T(8,128)S(1)} %multiply_add_fusion.7), channel_id=1, source_target_pairs={{0,128},{8,136},{16,144},{24,152},{32,160},{40,168},{48,176},{56,1... | collective-permute-start | bytes 491528 | tf_op jit(solution)/shard_map/ppermute | solution.py:9
  120.3 28.6 %copy-start.57 = (f32[5]{0:T(128)S(1)}, f32[5]{0:T(128)}, u32[]{:S(2)}) copy-start(f32[5]{0:T(128)} %dynamic_slice.61) | copy-start | bytes 64
  120.3 28.6 %copy-start.58 = (f32[5]{0:T(128)S(1)}, f32[5]{0:T(128)}, u32[]{:S(2)}) copy-start(f32[5]{0:T(128)} %dynamic_slice.62) | copy-start | bytes 64
  120.3 36.7 %copy-start.30 = (f32[10]{0:T(128)S(1)}, f32[10]{0:T(128)}, u32[]{:S(2)}) copy-start(f32[10]{0:T(128)} %copy-done.29) | copy-start | bytes 124
  120.3 36.7 %copy-start.42 = (f32[10]{0:T(128)S(1)}, f32[10]{0:T(128)}, u32[]{:S(2)}) copy-start(f32[10]{0:T(128)} %copy-done.41) | copy-start | bytes 124
  120.3 52.1 %collective-permute-start.4 = (f32[3,5,64,128]{3,2,1,0:T(8,128)S(1)}, f32[3,5,64,128]{3,2,1,0:T(8,128)S(1)}, u32[]{:S(2)}, u32[]{:S(2)}) collective-permute-start(f32[3,5,64,128]{3,2,1,0:T(8,128)S(1)} %pad_maximum_fusion), channel_id=1, source_target_pairs={{0,8},{8,0},{16,24},{24,16},{32,40},{40,32},{48,56},{56,48},{64,72... | collective-permute-start | bytes 1474568 | tf_op jit(solution)/shard_map/ppermute | solution.py:9
  147.0 10.1 %collective-permute-start.17 = (f32[10,32,128]{2,1,0:T(8,128)S(1)}, f32[10,32,128]{2,1,0:T(8,128)S(1)}, u32[]{:S(2)}, u32[]{:S(2)}) collective-permute-start(f32[10,32,128]{2,1,0:T(8,128)S(1)} %get-tuple-element.146), channel_id=1, source_target_pairs={{0,32},{8,40},{16,48},{24,56},{32,0},{40,8},{48,16},{56,24},{64,96... | collective-permute-start | bytes 491528 | tf_op jit(solution)/shard_map/ppermute | solution.py:9
  149.0 11.0 %collective-permute-start.6 = (f32[5,64,128]{2,1,0:T(8,128)S(1)}, f32[5,64,128]{2,1,0:T(8,128)S(1)}, u32[]{:S(2)}, u32[]{:S(2)}) collective-permute-start(f32[5,64,128]{2,1,0:T(8,128)S(1)} %multiply_add_fusion.6), channel_id=1, source_target_pairs={{0,256},{8,264},{16,272},{24,280},{32,288},{40,296},{48,304},{56,3... | collective-permute-start | bytes 491528 | tf_op jit(solution)/shard_map/ppermute | solution.py:9
  158.1 8.7 %collective-permute-start.18 = (f32[10,32,128]{2,1,0:T(8,128)S(1)}, f32[10,32,128]{2,1,0:T(8,128)S(1)}, u32[]{:S(2)}, u32[]{:S(2)}) collective-permute-start(f32[10,32,128]{2,1,0:T(8,128)S(1)} %fusion.74), channel_id=1, source_target_pairs={{0,16},{8,24},{16,0},{24,8},{32,48},{40,56},{48,32},{56,40},{64,80... | collective-permute-start | bytes 491528 | tf_op jit(solution)/shard_map/ppermute | solution.py:9
  160.2 10.1 %collective-permute-start.8 = (f32[5,64,128]{2,1,0:T(8,128)S(1)}, f32[5,64,128]{2,1,0:T(8,128)}, u32[]{:S(2)}, u32[]{:S(2)}) collective-permute-start(f32[5,64,128]{2,1,0:T(8,128)S(1)} %multiply_add_fusion.5), channel_id=1, source_target_pairs={{0,512},{8,520},{16,528},{24,536},{32,544},{40,552},{48,560},{56,5... | collective-permute-start | bytes 491528 | tf_op jit(solution)/shard_map/ppermute | solution.py:9
  164.4 42.9 %collective-permute-start.7 = (f32[2,5,64,128]{3,2,1,0:T(8,128)}, f32[2,5,64,128]{3,2,1,0:T(8,128)}, u32[]{:S(2)}, u32[]{:S(2)}) collective-permute-start(f32[2,5,64,128]{3,2,1,0:T(8,128)} %pad_maximum_fusion.2), channel_id=1, source_target_pairs={{0,8},{8,0},{16,24},{24,16},{32,40},{40,32},{48,56},{56,48},{64,72... | collective-permute-start | bytes 983048 | tf_op jit(solution)/shard_map/ppermute | solution.py:9
  166.9 12.2 %collective-permute-start.19 = (f32[10,32,128]{2,1,0:T(8,128)S(1)}, f32[10,32,128]{2,1,0:T(8,128)S(1)}, u32[]{:S(2)}, u32[]{:S(2)}) collective-permute-start(f32[10,32,128]{2,1,0:T(8,128)S(1)} %multiply_add_fusion), channel_id=1, source_target_pairs={{0,8},{8,0},{16,24},{24,16},{32,40},{40,32},{48,56},{56,48},{64,72... | collective-permute-start | bytes 491528 | tf_op jit(solution)/shard_map/ppermute | solution.py:9
  170.3 35.5 %collective-permute-start.9 = (f32[1,5,64,128]{3,2,1,0:T(8,128)}, f32[1,5,64,128]{3,2,1,0:T(8,128)}, u32[]{:S(2)}, u32[]{:S(2)}) collective-permute-start(f32[1,5,64,128]{3,2,1,0:T(8,128)} %bitcast.43), channel_id=1, source_target_pairs={{0,8},{8,0},{16,24},{24,16},{32,40},{40,32},{48,56},{56,48},{64,72... | collective-permute-start | bytes 491528 | tf_op jit(solution)/shard_map/ppermute | solution.py:9
  180.6 19.3 %copy-start.17 = (f32[10,256]{1,0:T(8,128)S(1)}, f32[10,256]{1,0:T(8,128)}, u32[]{:S(2)}) copy-start(f32[10,256]{1,0:T(8,128)} %copy-done.16) | copy-start | bytes 30724
  181.4 23.8 %all-to-all-start.2 = ((f32[8,32,128]{2,1,0:T(8,128)}), f32[8,32,128]{2,1,0:T(8,128)S(1)}, u32[]{:S(2)}, u32[]{:S(2)}) async-start(f32[8,32,128]{2,1,0:T(8,128)} %bitcast.66), calls=%async_computation.2 | async-start | bytes 262144 | tf_op jit(solution)/shard_map/all_to_all | solution.py:19
  211.3 9.4 %all-to-all-start.3 = ((f32[8,32,128]{2,1,0:T(8,128)}), f32[8,32,128]{2,1,0:T(8,128)S(1)}, u32[]{:S(2)}, u32[]{:S(2)}) async-start(f32[8,32,128]{2,1,0:T(8,128)} %bitcast.74), calls=%async_computation.3 | async-start | bytes 262144 | tf_op jit(solution)/shard_map/all_to_all | solution.py:19
  (40 other events, 201.3 us)
